TPU v7x, 32 devices: a whole 2x2x4 slice. The times are simulated.
32 devices in a mesh: seq: 4 (over x, core), dp: 8 (over z, y).
Axes of the slice: x: 2, y: 2, z: 4, core: 2. Of those that a mesh axis runs over, the one named last changes fastest.
Arguments:
- tokens: bfloat16 [8, 2048, 1024], P('dp', 'seq'), may hold values from -6 to 6
- lengths: int32 [8, 3], P('dp'), may hold values from 1 to 2046, as said below
- attend_weight: bfloat16 [1024, 3072], P('dp'), may hold values from -0.1875 to 0.1875
- output_weight: bfloat16 [1024, 1024], P('dp'), may hold values from -3 to 3
- expand_weight: bfloat16 [1024, 4096], P('dp'), may hold values from -0.1875 to 0.1875
- shrink_weight: bfloat16 [4096, 1024], P('dp'), may hold values from -0.09375 to 0.09375
- prefix_embed: float32 [10, 1024], replicated, may hold values from -6 to 6
- inner_weight: float32 [1024, 512], replicated, may hold values from -0.1875 to 0.1875
- inner_bias: float32 [512], replicated, may hold values from -3 to 3
- outer_weight: float32 [512, 2048], replicated, may hold values from -0.25 to 0.25
- outer_bias: float32 [2048], replicated, may hold values from -3 to 3
- cotangent: bfloat16 [8, 2048, 1024], P('dp', 'seq'), may hold values from -6 to 6
Outputs:
- outputs: bfloat16 [8, 2048, 1024], P('dp', 'seq')
- grad_tokens: bfloat16 [8, 2048, 1024], P('dp', 'seq')
- embed_grad: float32 [10, 1024], replicated
- inner_grad: float32 [1024, 512], replicated
- inner_bias_grad: float32 [512], replicated
- outer_grad: float32 [512, 2048], replicated
- outer_bias_grad: float32 [2048], replicated
- prefix_kv: float32 [10, 2048], replicated
Inputs may be any that keep to these rules, and one draw needn't show every extreme that they name: `lengths`: each row sums to 2048; in each row one document is longer than 1536 tokens and the others hold at most 128 tokens.
All inputs are finite; a program needn't handle non-finite values.
Results may differ from a plain program's by a relative error of at most 0.024.
Values may be sent and summed in bfloat16 or wider, within the bound.
No kernel may reach another device: no remote copies, remote signals or barrier semaphores. Data moves between devices by JAX's collectives and lax.ppermute only.
A program may use at most 256 MiB of HBM per device.

v0:
```python
import math

import jax
import jax.numpy as jnp
from jax import lax
from jax.sharding import PartitionSpec as P

HEADS = 16
HEAD_DIM = 64
PREFIX = 10


norm_epsilon = 1e-05
masked_value = -1e30
highest = lax.Precision.HIGHEST


def layer_norm(hidden):
    centered = hidden - jnp.mean(hidden, axis=-1, keepdims=True)
    return centered * lax.rsqrt(
        jnp.mean(centered * centered, axis=-1, keepdims=True) + norm_epsilon
    )


def gelu_tanh(values):
    return (
        0.5
        * values
        * (1.0 + jnp.tanh(0.7978845608028654 * (values + 0.044715 * values * values * values)))
    )


def document_ids(lengths_row, positions):
    doc_ends = jnp.cumsum(lengths_row)
    return jnp.sum((positions[:, None] >= doc_ends[None, :]).astype(jnp.int32), axis=1)


def times_transposed(left, right):
    return lax.dot_general(
        left, right, (((1,), (1,)), ((), ())), preferred_element_type=jnp.float32
    )


def reparam(embedding, inner_matrix, inner_shift, outer_matrix, outer_shift):
    hidden = jnp.tanh(
        jnp.dot(embedding, inner_matrix, precision=highest, preferred_element_type=jnp.float32)
        + inner_shift
    )
    return (
        jnp.dot(hidden, outer_matrix, precision=highest, preferred_element_type=jnp.float32)
        + outer_shift
    )


def pair_grads(
    query_part,
    out_part,
    total_part,
    delta_part,
    query_pos,
    query_doc,
    key_part,
    value_part,
    key_pos,
    key_doc,
    scale,
):
    allowed = (key_doc[None, :] == query_doc[:, None]) & (key_pos[None, :] <= query_pos[:, None])
    scores = (
        jnp.einsum("qhd,khd->hqk", query_part, key_part, preferred_element_type=jnp.float32) * scale
    )
    scores = jnp.where(allowed[None], scores, masked_value)
    probs = jnp.exp(scores - total_part[:, :, None])
    prob_grad = jnp.einsum("qhd,khd->hqk", out_part, value_part, preferred_element_type=jnp.float32)
    score_grad = (probs * (prob_grad - delta_part[:, :, None])).astype(jnp.bfloat16)
    return (probs, score_grad)


def shards(
    tokens,
    lengths,
    attend_weight,
    output_weight,
    expand_weight,
    shrink_weight,
    prefix_embed,
    inner_weight,
    inner_bias,
    outer_weight,
    outer_bias,
    cotangent,
):
    token_rows = tokens[0].astype(jnp.float32)
    row_count = token_rows.shape[0]
    model_width = token_rows.shape[1]
    head_count = HEADS
    head_size = HEAD_DIM
    scale = 1.0 / math.sqrt(head_size)
    lengths_row = lengths[0]
    first_row = lax.axis_index("seq") * row_count
    query_pos = first_row + jnp.arange(row_count, dtype=jnp.int32)
    query_doc = document_ids(lengths_row, query_pos)
    last_query = first_row + row_count - 1
    full_attend, full_output, full_expand, full_shrink = (
        lax.all_gather(attend_weight, "dp", axis=0, tiled=True),
        lax.all_gather(output_weight, "dp", axis=0, tiled=True),
        lax.all_gather(expand_weight, "dp", axis=0, tiled=True),
        lax.all_gather(shrink_weight, "dp", axis=0, tiled=True),
    )
    prefix_kv, reparam_back = jax.vjp(
        reparam, prefix_embed, inner_weight, inner_bias, outer_weight, outer_bias
    )
    prefix_keys = (
        prefix_kv[:, :model_width].astype(jnp.bfloat16).reshape(PREFIX, head_count, head_size)
    )
    prefix_values = (
        prefix_kv[:, model_width:].astype(jnp.bfloat16).reshape(PREFIX, head_count, head_size)
    )
    normed_full, input_norm_back = jax.vjp(layer_norm, token_rows)
    projected = jnp.dot(
        normed_full.astype(jnp.bfloat16), full_attend, preferred_element_type=jnp.float32
    )
    queries = (
        projected[:, :model_width].astype(jnp.bfloat16).reshape(row_count, head_count, head_size)
    )
    key_rows = projected[:, model_width : 2 * model_width].astype(jnp.bfloat16)
    value_rows = projected[:, 2 * model_width :].astype(jnp.bfloat16)
    prefix_scores = (
        jnp.einsum("qhd,phd->hqp", queries, prefix_keys, preferred_element_type=jnp.float32) * scale
    )
    start_max = jnp.max(prefix_scores, axis=2)
    start_exp = jnp.exp(prefix_scores - start_max[:, :, None])
    start_sum = jnp.sum(start_exp, axis=2)
    start_acc = jnp.einsum(
        "hqp,phd->qhd",
        start_exp.astype(jnp.bfloat16),
        prefix_values,
        preferred_element_type=jnp.float32,
    )

    def key_block(running, key_piece, value_piece, key_start):
        run_max, run_sum, run_acc = running
        piece_rows = key_piece.shape[0]
        key_pos = key_start + jnp.arange(piece_rows, dtype=jnp.int32)
        key_doc = document_ids(lengths_row, key_pos)
        allowed = (key_doc[None, :] == query_doc[:, None]) & (
            key_pos[None, :] <= query_pos[:, None]
        )
        scores = (
            jnp.einsum(
                "qhd,khd->hqk",
                queries,
                key_piece.reshape(piece_rows, head_count, head_size),
                preferred_element_type=jnp.float32,
            )
            * scale
        )
        scores = jnp.where(allowed[None], scores, masked_value)
        new_max = jnp.maximum(run_max, jnp.max(scores, axis=2))
        factor = jnp.exp(run_max - new_max)
        exps = jnp.exp(scores - new_max[:, :, None])
        new_sum = run_sum * factor + jnp.sum(exps, axis=2)
        new_acc = run_acc * factor.T[:, :, None] + jnp.einsum(
            "hqk,khd->qhd",
            exps.astype(jnp.bfloat16),
            value_piece.reshape(piece_rows, head_count, head_size),
            preferred_element_type=jnp.float32,
        )
        return (new_max, new_sum, new_acc)

    running = (start_max, start_sum, start_acc)
    key_piece = lax.all_gather(key_rows, "seq", axis=0, tiled=True)
    value_piece = lax.all_gather(value_rows, "seq", axis=0, tiled=True)
    piece_rows = key_piece.shape[0]

    def step(state_now, block_index):
        key_part = lax.dynamic_slice_in_dim(key_piece, block_index * 512, 512, 0)
        value_part = lax.dynamic_slice_in_dim(value_piece, block_index * 512, 512, 0)
        return (key_block(state_now, key_part, value_part, block_index * 512), None)

    running, unused = lax.scan(step, running, jnp.arange(piece_rows // 512, dtype=jnp.int32))
    run_max, run_sum, run_acc = running
    log_total = run_max + jnp.log(run_sum)
    attended = run_acc / run_sum.T[:, :, None]
    merged = attended.reshape(row_count, model_width).astype(jnp.bfloat16)
    residual_mid = token_rows + jnp.dot(merged, full_output, preferred_element_type=jnp.float32)
    normed_mid, mid_norm_back = jax.vjp(layer_norm, residual_mid)
    expanded = jnp.dot(
        normed_mid.astype(jnp.bfloat16), full_expand, preferred_element_type=jnp.float32
    )
    activated_full, gelu_back = jax.vjp(gelu_tanh, expanded)
    outputs = residual_mid + jnp.dot(
        activated_full.astype(jnp.bfloat16), full_shrink, preferred_element_type=jnp.float32
    )
    back_attend, back_output, back_expand, back_shrink = (
        lax.all_gather(attend_weight, "dp", axis=0, tiled=True),
        lax.all_gather(output_weight, "dp", axis=0, tiled=True),
        lax.all_gather(expand_weight, "dp", axis=0, tiled=True),
        lax.all_gather(shrink_weight, "dp", axis=0, tiled=True),
    )
    upstream = cotangent[0]
    gelu_grad = times_transposed(upstream, back_shrink)
    expand_grad = gelu_back(gelu_grad)[0].astype(jnp.bfloat16)
    normed_grad = times_transposed(expand_grad, back_expand)
    mid_grad = upstream.astype(jnp.float32) + mid_norm_back(normed_grad)[0]
    out_grad = times_transposed(mid_grad.astype(jnp.bfloat16), back_output).astype(jnp.bfloat16)
    out_heads = out_grad.reshape(row_count, head_count, head_size)
    row_delta = jnp.sum(out_heads.astype(jnp.float32) * attended, axis=2).T
    prefix_probs = jnp.exp(prefix_scores - log_total[:, :, None])
    prefix_prob_grad = jnp.einsum(
        "qhd,phd->hqp", out_heads, prefix_values, preferred_element_type=jnp.float32
    )
    prefix_score_grad = (prefix_probs * (prefix_prob_grad - row_delta[:, :, None])).astype(
        jnp.bfloat16
    )
    query_start = (
        jnp.einsum(
            "hqp,phd->qhd", prefix_score_grad, prefix_keys, preferred_element_type=jnp.float32
        )
        * scale
    )
    prefix_key_grad = (
        jnp.einsum("hqp,qhd->phd", prefix_score_grad, queries, preferred_element_type=jnp.float32)
        * scale
    )
    prefix_value_grad = jnp.einsum(
        "hqp,qhd->phd",
        prefix_probs.astype(jnp.bfloat16),
        out_heads,
        preferred_element_type=jnp.float32,
    )
    all_keys, all_values = (
        lax.all_gather(key_rows, "seq", axis=0, tiled=True),
        lax.all_gather(value_rows, "seq", axis=0, tiled=True),
    )
    total_rows = all_keys.shape[0]
    key_block_rows = min(512, total_rows)
    block_ids = jnp.arange(total_rows // key_block_rows, dtype=jnp.int32)

    def key_slices(block_index):
        key_part = lax.dynamic_slice_in_dim(
            all_keys, block_index * key_block_rows, key_block_rows, 0
        ).reshape(key_block_rows, head_count, head_size)
        value_part = lax.dynamic_slice_in_dim(
            all_values, block_index * key_block_rows, key_block_rows, 0
        ).reshape(key_block_rows, head_count, head_size)
        key_pos = block_index * key_block_rows + jnp.arange(key_block_rows, dtype=jnp.int32)
        return (key_part, value_part, key_pos, document_ids(lengths_row, key_pos))

    def back_block(query_acc, block_index):

        def compute(unused):
            key_part, value_part, key_pos, key_doc = key_slices(block_index)
            probs, score_grad = pair_grads(
                queries,
                out_heads,
                log_total,
                row_delta,
                query_pos,
                query_doc,
                key_part,
                value_part,
                key_pos,
                key_doc,
                scale,
            )
            query_term = (
                jnp.einsum("hqk,khd->qhd", score_grad, key_part, preferred_element_type=jnp.float32)
                * scale
            )
            key_grad = (
                jnp.einsum("hqk,qhd->khd", score_grad, queries, preferred_element_type=jnp.float32)
                * scale
            )
            value_grad = jnp.einsum(
                "hqk,qhd->khd",
                probs.astype(jnp.bfloat16),
                out_heads,
                preferred_element_type=jnp.float32,
            )
            joined = jnp.concatenate(
                [
                    key_grad.reshape(key_block_rows, model_width),
                    value_grad.reshape(key_block_rows, model_width),
                ],
                axis=1,
            )
            return (query_term, joined)

        def skipped(unused):
            return (
                jnp.zeros((row_count, head_count, head_size), jnp.float32),
                jnp.zeros((key_block_rows, 2 * model_width), jnp.float32),
            )

        query_term, joined = lax.cond(
            block_index * key_block_rows <= last_query, compute, skipped, 0
        )
        return (query_acc + query_term, joined)

    query_total, key_terms = lax.scan(back_block, query_start, block_ids)
    key_terms = key_terms.reshape(total_rows, 2 * model_width)
    key_value_grad = lax.psum_scatter(
        key_terms.astype(jnp.bfloat16), "seq", scatter_dimension=0, tiled=True
    ).astype(jnp.float32)
    projected_grad = jnp.concatenate(
        [query_total.reshape(row_count, model_width), key_value_grad], axis=1
    ).astype(jnp.bfloat16)
    input_grad = mid_grad + input_norm_back(times_transposed(projected_grad, back_attend))[0]
    prefix_grad = jnp.concatenate(
        [
            prefix_key_grad.reshape(PREFIX, model_width),
            prefix_value_grad.reshape(PREFIX, model_width),
        ],
        axis=1,
    )
    local_grads = reparam_back(prefix_grad)
    summed = lax.psum(
        (local_grads[0], local_grads[1], local_grads[2], local_grads[3], local_grads[4]),
        ("seq", "dp"),
    )
    return (
        outputs.astype(jnp.bfloat16)[None],
        input_grad.astype(jnp.bfloat16)[None],
        summed[0],
        summed[1],
        summed[2],
        summed[3],
        summed[4],
        prefix_kv,
    )


def solution(mesh):
    placed = (
        P("dp", "seq", None),
        P("dp", None),
        P("dp", None),
        P("dp", None),
        P("dp", None),
        P("dp", None),
        P(),
        P(),
        P(),
        P(),
        P(),
        P("dp", "seq", None),
    )
    return jax.shard_map(
        shards,
        mesh=mesh,
        in_specs=placed,
        out_specs=(P("dp", "seq", None), P("dp", "seq", None), P(), P(), P(), P(), P(), P()),
        check_vma=False,
    )
```

profile of v0, /device:TPU:0, one launch (start us, length us, event | category | flops | bytes accessed | tf_op | source)
XLA Modules:
  0.0 872.6 jit_solution(13613680797821246310)
XLA Ops:
  11.7 100.3 %all-gather.7.cloned.1.call-done = bf16[1024,3072]{1,0:T(8,128)(2,1)} async-done(((bf16[128,3072]{1,0:T(8,128)(2,1)}), bf16[1024,3072]{1,0:T(8,128)(2,1)}) %all-gather.7.cloned.1.call-update) | async-done | bytes 6291472 | tf_op jit(solution)/shard_map/all_gather | solution.py:105
  112.0 6.6 convolution_convert_fusion
  124.0 5.4 fusion.95
  135.7 17.4 %all-gather.9.cloned.1.call-done = bf16[2048,1024]{1,0:T(8,128)(2,1)} async-done(((bf16[512,1024]{1,0:T(8,128)(2,1)}), bf16[2048,1024]{1,0:T(8,128)(2,1)}) %all-gather.9.cloned.1.call-update) | async-done | bytes 4194320 | tf_op jit(solution)/shard_map/all_gather | solution.py:172
  153.1 6.4 copy.87
  159.6 30.3 %all-gather.11.cloned.1.call-done = bf16[2048,1024]{1,0:T(8,128)(2,1)} async-done(((bf16[512,1024]{1,0:T(8,128)(2,1)}), bf16[2048,1024]{1,0:T(8,128)(2,1)}) %all-gather.11.cloned.1.call-update) | async-done | bytes 4194320 | tf_op jit(solution)/shard_map/all_gather | solution.py:173
  189.8 6.5 copy.88
  196.3 128.5 %while.30 = (s32[]{:T(128)}, f32[16,512]{1,0:T(8,128)S(1)}, f32[16,512]{1,0:T(8,128)S(1)}, f32[512,16,64]{0,2,1:T(8,128)}, s32[4]{0:T(128)S(1)}, /*index=5*/s32[...) while((s32[]{:T(128)}, f32[16,512]{1,0:T(8,128)S(1)}, ...), condition=%wide.region_11.12_spmd.clone, body=%wide.region_7.11_spmd.clone.sunk | while | flops 1121743872 | bytes 63455464 | solution.py:181
  199.7 8.6 fusion.154
  208.9 9.2 %fusion.156 = f32[16,512]{1,0:T(8,128)S(1)} fusion(f32[16,512,512]{2,1,0:T(8,128)} %get-tuple-element.680, f32[16,512]{1,0:T(8,128)S(1)} %get-tuple-element.734, pred[512,512]{0,1:T(8,128)(4,1)S(1)} %compare_and_fusion.3), kind=kLoop, calls=%fused_computation.24.clone.1 | loop fusion | flops 16769024 | bytes 17104896 | tf_op jit(solution)/shard_map/while/body/eval_jaxpr/reduce_sum | solution.py:162
  218.1 10.2 %bitcast_add_fusion.2 = f32[512,16,64]{0,2,1:T(8,128)} fusion(f32[512,16,64]{0,2,1:T(8,128)} %get-tuple-element.721, bf16[512,16,64]{0,2,1:T(8,128)(2,1)S(1)} %bitcast.183, f32[16,512,512]{2,1,0:T(8,128)} %get-tuple-element.680, f32[16,512]{1,0:T(8,128)S(1)} %get-tuple-element.734, pred[512,512]{0,1:T(8,128)(4,1)S(1)} %compare_and_fusion.3, ...), kind=kOutput, calls=%fused_computation.28.clone.1 | convolution fusion | flops 554696704 | bytes 22347776 | tf_op jit(solution)/shard_map/while/body/eval_jaxpr/hqk,khd->qhd/dot_general | solution.py:163
  231.7 8.5 fusion.154
  240.8 9.2 %fusion.156 = f32[16,512]{1,0:T(8,128)S(1)} fusion(f32[16,512,512]{2,1,0:T(8,128)} %get-tuple-element.680, f32[16,512]{1,0:T(8,128)S(1)} %get-tuple-element.734, pred[512,512]{0,1:T(8,128)(4,1)S(1)} %compare_and_fusion.3), kind=kLoop, calls=%fused_computation.24.clone.1 | loop fusion | flops 16769024 | bytes 17104896 | tf_op jit(solution)/shard_map/while/body/eval_jaxpr/reduce_sum | solution.py:162
  250.0 10.5 %bitcast_add_fusion.2 = f32[512,16,64]{0,2,1:T(8,128)} fusion(f32[512,16,64]{0,2,1:T(8,128)} %get-tuple-element.721, bf16[512,16,64]{0,2,1:T(8,128)(2,1)S(1)} %bitcast.183, f32[16,512,512]{2,1,0:T(8,128)} %get-tuple-element.680, f32[16,512]{1,0:T(8,128)S(1)} %get-tuple-element.734, pred[512,512]{0,1:T(8,128)(4,1)S(1)} %compare_and_fusion.3, ...), kind=kOutput, calls=%fused_computation.28.clone.1 | convolution fusion | flops 554696704 | bytes 22347776 | tf_op jit(solution)/shard_map/while/body/eval_jaxpr/hqk,khd->qhd/dot_general | solution.py:163
  263.8 8.5 fusion.154
  273.0 9.2 %fusion.156 = f32[16,512]{1,0:T(8,128)S(1)} fusion(f32[16,512,512]{2,1,0:T(8,128)} %get-tuple-element.680, f32[16,512]{1,0:T(8,128)S(1)} %get-tuple-element.734, pred[512,512]{0,1:T(8,128)(4,1)S(1)} %compare_and_fusion.3), kind=kLoop, calls=%fused_computation.24.clone.1 | loop fusion | flops 16769024 | bytes 17104896 | tf_op jit(solution)/shard_map/while/body/eval_jaxpr/reduce_sum | solution.py:162
  282.3 10.1 %bitcast_add_fusion.2 = f32[512,16,64]{0,2,1:T(8,128)} fusion(f32[512,16,64]{0,2,1:T(8,128)} %get-tuple-element.721, bf16[512,16,64]{0,2,1:T(8,128)(2,1)S(1)} %bitcast.183, f32[16,512,512]{2,1,0:T(8,128)} %get-tuple-element.680, f32[16,512]{1,0:T(8,128)S(1)} %get-tuple-element.734, pred[512,512]{0,1:T(8,128)(4,1)S(1)} %compare_and_fusion.3, ...), kind=kOutput, calls=%fused_computation.28.clone.1 | convolution fusion | flops 554696704 | bytes 22347776 | tf_op jit(solution)/shard_map/while/body/eval_jaxpr/hqk,khd->qhd/dot_general | solution.py:163
  294.0 1.9 constant_dynamic-slice_fusion.5
  295.9 8.5 fusion.154
  305.1 9.3 %fusion.156 = f32[16,512]{1,0:T(8,128)S(1)} fusion(f32[16,512,512]{2,1,0:T(8,128)} %get-tuple-element.680, f32[16,512]{1,0:T(8,128)S(1)} %get-tuple-element.734, pred[512,512]{0,1:T(8,128)(4,1)S(1)} %compare_and_fusion.3), kind=kLoop, calls=%fused_computation.24.clone.1 | loop fusion | flops 16769024 | bytes 17104896 | tf_op jit(solution)/shard_map/while/body/eval_jaxpr/reduce_sum | solution.py:162
  314.4 10.2 %bitcast_add_fusion.2 = f32[512,16,64]{0,2,1:T(8,128)} fusion(f32[512,16,64]{0,2,1:T(8,128)} %get-tuple-element.721, bf16[512,16,64]{0,2,1:T(8,128)(2,1)S(1)} %bitcast.183, f32[16,512,512]{2,1,0:T(8,128)} %get-tuple-element.680, f32[16,512]{1,0:T(8,128)S(1)} %get-tuple-element.734, pred[512,512]{0,1:T(8,128)(4,1)S(1)} %compare_and_fusion.3, ...), kind=kOutput, calls=%fused_computation.28.clone.1 | convolution fusion | flops 554696704 | bytes 22347776 | tf_op jit(solution)/shard_map/while/body/eval_jaxpr/hqk,khd->qhd/dot_general | solution.py:163
  324.8 1.9 fusion.68
  326.7 3.2 fusion.97
  331.6 35.0 %all-gather.15.cloned.1.call-done = bf16[1024,4096]{1,0:T(8,128)(2,1)} async-done(((bf16[128,4096]{1,0:T(8,128)(2,1)}), bf16[1024,4096]{1,0:T(8,128)(2,1)}) %all-gather.15.cloned.1.call-update) | async-done | bytes 8388624 | tf_op jit(solution)/shard_map/all_gather | solution.py:107
  366.6 11.8 %fusion.53 = f32[512,4096]{1,0:T(8,128)} fusion(bf16[1024,4096]{1,0:T(8,128)(2,1)} %all-gather.15.cloned.1.call-done, f32[512,1024]{1,0:T(8,128)} %copy-done.3, f32[512]{0:T(512)S(1)} %fusion.81, f32[512]{0:T(512)S(1)} %broadcast_multiply_fusion), kind=kOutput, calls=%fused_computation.96 | convolution fusion | flops 4296540160 | bytes 18878464 | tf_op jit(solution)/shard_map/dot_general | solution.py:188
  378.4 113.3 %all-gather.17.cloned.1.call-done = bf16[4096,1024]{1,0:T(8,128)(2,1)} async-done(((bf16[512,1024]{1,0:T(8,128)(2,1)}), bf16[4096,1024]{1,0:T(8,128)(2,1)}) %all-gather.17.cloned.1.call-update) | async-done | bytes 8388624 | tf_op jit(solution)/shard_map/all_gather | solution.py:108
  491.7 18.9 %multiply_reduce_fusion.1 = (f32[512]{0:T(512)S(1)}, f32[512,1024]{1,0:T(8,128)}) fusion(f32[512,1024]{1,0:T(8,128)} %copy-done.3, f32[512]{0:T(512)S(1)} %broadcast_multiply_fusion, bf16[1024,4096]{1,0:T(8,128)(2,1)} %all-gather.15.cloned.1.call-done, f32[512,4096]{1,0:T(8,128)} %fusion.53, bf16[4096,1024]{1,0:T(8,128)(2,1)} %all-gather.17.cloned.1.call-done, ...), kind=kOutput, calls=%fused_computation.77 | convolution fusion | flops 8641839104 | bytes 30412800 | tf_op jit(solution)/shard_map/dot_general | solution.py:39
  510.6 3.0 fusion.92
  515.0 2.3 convolution_convert_fusion.1
  517.3 2.7 copy.89
  520.0 2.3 multiply_reduce_fusion
  527.4 6.3 fusion.100
  533.7 5.1 fusion.103
  538.8 3.2 convolution_bitcast_fusion
  543.8 107.5 %while.31 = (s32[]{:T(128)}, f32[512,16,64]{0,2,1:T(8,128)}, bf16[4,512,2048]{2,1,0:T(8,128)(2,1)}, s32[4]{0:T(128)S(1)}, s32[]{:T(128)}, /*index=5*/bf16[2048,1...) while((s32[]{:T(128)}, f32[512,16,64]{0,2,1:T(8,128)}, ...), condition=%wide.region_22.23_spmd.clone, body=%wide.region_17.0_spmd.clone.sunk | while | flops 2733380608 | bytes 144560560 | solution.py:301
  545.4 47.2 %conditional.3 = (f32[512,16,64]{0,2,1:T(8,128)}, bf16[1,512,2048]{1,2,0:T(8,128)(2,1)}) conditional(s32[]{:T(128)} %convert_element_type.192, () %tuple.98, (s32[]{:T(128)}, bf16[2048,1024]{0,1:T(8,128)(2,1)}, s32[3]{0:T(128)S(1)}, s32[512]{0:T(512)S(1)}, s32[]{:T(128)}, /*index=5*/bf16[512,16,64]{0,2,1:T(8,128)(2,1)}, f32[16,512]{1,0:T(8,128)S(1)}, ...), branch_computations={%region_18.18_spmd, %region_19.21_spmd} | conditional | flops 2732856320 | bytes 129878152 | solution.py:296
  546.1 2.8 constant_dynamic-slice_fusion
  548.8 9.4 %fusion.101 = f32[16,512,512]{2,1,0:T(8,128)} fusion(bf16[512,16,64]{0,2,1:T(8,128)(2,1)S(1)} %bitcast.180, bf16[512,16,64]{0,2,1:T(8,128)(2,1)} %get-tuple-element.208), kind=kOutput, calls=%fused_computation.151 | convolution fusion | flops 536870912 | bytes 18874368 | tf_op jit(solution)/shard_map/while/body/eval_jaxpr/cond/branch_1_fun/qhd,khd->hqk/dot_general | solution.py:70
  558.8 9.7 %fusion.4 = bf16[16,512,512]{1,2,0:T(8,128)(2,1)S(1)} fusion(f32[16,512,512]{2,1,0:T(8,128)} %fusion.101, bf16[512,16,64]{0,2,1:T(8,128)(2,1)} %bitcast.184, bf16[512,16,64]{0,2,1:T(8,128)(2,1)} %get-tuple-element.211, f32[16,512]{1,0:T(8,128)S(1)} %get-tuple-element.212, f32[16,512]{1,0:T(8,128)S(1)} %get-tuple-element.209, ...), kind=kOutput, calls=%fused_computation.3 | convolution fusion | flops 562036736 | bytes 27590656 | tf_op jit(solution)/shard_map/while/body/eval_jaxpr/cond/branch_1_fun/qhd,khd->hqk/dot_general | solution.py:74
  568.5 3.2 copy-done.1
  571.7 2.8 multiply_bitcast_fusion
  574.5 10.4 %fusion.8 = bf16[16,512,64]{1,2,0:T(8,128)(2,1)S(1)} fusion(bf16[512,16,64]{0,2,1:T(8,128)(2,1)} %get-tuple-element.211, f32[16,512,512]{2,1,0:T(8,128)} %fusion.101, f32[16,512]{1,0:T(8,128)S(1)} %get-tuple-element.209, pred[512,512]{0,1:T(8,128)(4,1)S(1)} %compare_and_fusion), kind=kOutput, calls=%fused_computation.8 | convolution fusion | flops 553648128 | bytes 19169280 | tf_op jit(solution)/shard_map/while/body/eval_jaxpr/cond/branch_1_fun/hqk,qhd->khd/dot_general | solution.py:275
  584.9 6.3 convolution_multiply_fusion
  592.6 4.1 add.283
  596.8 4.0 copy.128
  600.7 3.2 constant_dynamic-update-slice_fusion.4
  605.2 3.1 conditional.3
  608.3 4.1 add.283
  612.4 4.0 copy.128
  616.4 3.2 constant_dynamic-update-slice_fusion.4
  621.0 3.1 conditional.3
  624.1 4.1 add.283
  628.3 3.9 copy.128
  632.2 3.2 constant_dynamic-update-slice_fusion.4
  636.7 3.1 conditional.3
  639.8 4.2 add.283
  644.0 4.0 copy.128
  648.0 3.2 constant_dynamic-update-slice_fusion.4
  656.4 170.0 %all-reduce = (f32[10,1024]{1,0:T(8,128)}, f32[512]{0:T(512)}, f32[2048]{0:T(1024)}) all-reduce(f32[10,1024]{1,0:T(8,128)S(1)} %fusion.102, f32[512]{0:T(512)S(1)} %copy-done.35, f32[2048]{0:T(1024)S(1)} %reduce_sum.184), channel_id=1, replica_groups=mesh['seq'=4,'dp'=8] {'seq','dp'}, use_global_device_ids=true, to_apply=%region_26.27 | all-reduce | flops 12800 | bytes 102400 | tf_op jit(solution)/shard_map/psum | solution.py:318
  826.3 12.7 %fusion.46 = bf16[1,512,1024]{2,1,0:T(8,128)(2,1)} fusion(f32[512,1024]{1,0:T(8,128)} %copy-done.3, bf16[4096,1024]{1,0:T(8,128)(2,1)} %all-gather.17.cloned.1.call-done, f32[512,4096]{1,0:T(8,128)} %fusion.53), kind=kOutput, calls=%fused_computation.84 | convolution fusion | flops 4314890240 | bytes 19922944 | tf_op jit(solution)/shard_map/dot_general | solution.py:192
  839.0 3.0 copy.98
  842.0 11.4 %reduce-scatter.2.cloned.1.call-done = bf16[512,2048]{1,0:T(8,128)(2,1)} async-done(((bf16[2048,2048]{1,0:T(8,128)(2,1)}), bf16[512,2048]{1,0:T(8,128)(2,1)}) %reduce-scatter.2.cloned.1.call-update) | async-done | bytes 2097168 | tf_op jit(solution)/shard_map/reduce_scatter | solution.py:303
  853.4 6.7 fusion.45
  863.5 2.0 copy.160
  (191 shorter events, 59.8 us)
Async XLA Ops:
  7.2 115.7 %copy-start = (f32[1024,512]{1,0:T(8,128)S(1)}, f32[1024,512]{1,0:T(8,128)}, u32[]{:S(2)}) copy-start(f32[1024,512]{1,0:T(8,128)} %param.25) | copy-start | bytes 6291460
  7.2 104.8 %all-gather.7.cloned.1.call-start = ((), (), s32[]{:S(2)}) async-start(), calls=%async_computation.1 | async-start | bytes 7077888 | tf_op jit(solution)/shard_map/all_gather | solution.py:105
  7.9 145.2 %all-gather.9.cloned.1.call-start = ((), (), s32[]{:S(2)}) async-start(), calls=%async_computation.2 | async-start | bytes 5242880 | tf_op jit(solution)/shard_map/all_gather | solution.py:172
  9.4 102.6 %copy-start.28 = (f32[512]{0:T(512)}, f32[512]{0:T(512)S(1)}, u32[]{:S(2)}) copy-start(f32[512]{0:T(512)S(1)} %broadcast_multiply_fusion.1) | copy-start | bytes 6148
  11.1 0.6 copy-start.32
  11.7 100.3 %copy-start.30 = (f32[512]{0:T(512)}, f32[512]{0:T(512)S(1)}, u32[]{:S(2)}) copy-start(f32[512]{0:T(512)S(1)} %fusion.80) | copy-start | bytes 6148
  118.6 4.3 copy-start.24
  118.6 4.3 copy-start.38
  120.3 3.7 copy-start.34
  120.3 69.5 %all-gather.11.cloned.1.call-start = ((), (), s32[]{:S(2)}) async-start(), calls=%async_computation.3 | async-start | bytes 5242880 | tf_op jit(solution)/shard_map/all_gather | solution.py:173
  121.1 205.7 %all-gather.13.cloned.1.call-start = ((), (), s32[]{:S(2)}) async-start(), calls=%async_computation.4 | async-start | bytes 2359296 | tf_op jit(solution)/shard_map/all_gather | solution.py:106
  121.6 245.0 %all-gather.15.cloned.1.call-start = ((), (), s32[]{:S(2)}) async-start(), calls=%async_computation.5 | async-start | bytes 9437184 | tf_op jit(solution)/shard_map/all_gather | solution.py:107
  122.2 7.4 copy-start.39
  122.2 369.5 %all-gather.17.cloned.1.call-start = ((), (), s32[]{:S(2)}) async-start(), calls=%async_computation.6 | async-start | bytes 9437184 | tf_op jit(solution)/shard_map/all_gather | solution.py:108
  122.8 716.2 %all-reduce.4.cloned.1.call-start = ((), (), s32[]{:S(2)}) async-start(), calls=%async_computation.8 | async-start | bytes 12582912 | tf_op jit(solution)/shard_map/psum | solution.py:318
  124.0 5.4 copy-start.18
  129.5 30.0 %copy-start.14 = (bf16[10,16,64]{2,1,0:T(8,128)(2,1)}, bf16[10,16,64]{2,1,0:T(8,128)(2,1)S(1)}, u32[]{:S(2)}) copy-start(bf16[10,16,64]{2,1,0:T(8,128)(2,1)S(1)} %reshape.317) | copy-start | bytes 61444
  129.6 29.9 %copy-start.16 = (bf16[10,16,64]{2,1,0:T(8,128)(2,1)}, bf16[10,16,64]{2,1,0:T(8,128)(2,1)S(1)}, u32[]{:S(2)}) copy-start(bf16[10,16,64]{2,1,0:T(8,128)(2,1)S(1)} %reshape.318) | copy-start | bytes 61444
  133.1 0.8 copy-start.4
  329.9 1.3 copy-start.3
  331.6 160.1 %copy-start.12 = (bf16[1,512,1024]{2,1,0:T(8,128)(2,1)S(1)}, bf16[1,512,1024]{2,1,0:T(8,128)(2,1)}, u32[]{:S(2)}) copy-start(bf16[1,512,1024]{2,1,0:T(8,128)(2,1)} %param.29) | copy-start | bytes 3145732
  510.6 4.3 copy-start.9
  513.6 1.4 copy-start.6
  513.6 3.6 copy-start.36
  517.3 5.0 copy-start.5
  517.3 6.7 copy-start.17
  520.0 7.3 copy-start.19
  522.3 1.7 copy-start.26
  522.3 1.6 copy-start.22
  527.3 11.4 %copy-start.10 = (f32[10,2048]{1,0:T(8,128)}, f32[10,2048]{1,0:T(8,128)S(1)}, u32[]{:S(2)}) copy-start(f32[10,2048]{1,0:T(8,128)S(1)} %constant_dynamic-update-slice_fusion.1) | copy-start | bytes 245764
  527.3 11.4 %copy-start.25 = (f32[10,1024]{1,0:T(8,128)S(1)}, f32[10,1024]{1,0:T(8,128)}, u32[]{:S(2)}) copy-start(f32[10,1024]{1,0:T(8,128)} %param.24) | copy-start | bytes 122884
  533.7 8.3 copy-start.20
  538.8 3.3 copy-start.15
  541.9 1.9 copy-start.23
  541.9 1.9 copy-start.27
  542.0 311.4 %reduce-scatter.2.cloned.1.call-start = ((), (), s32[]{:S(2)}) async-start(), calls=%async_computation.7 | async-start | bytes 10485760 | tf_op jit(solution)/shard_map/reduce_scatter | solution.py:303
  568.5 3.2 copy-start.1
  651.4 3.2 copy-start.11
  651.4 3.2 copy-start.21
  651.4 5.0 copy-start.35
  839.0 14.3 %copy-start.2 = (bf16[1,512,1024]{2,1,0:T(8,128)(2,1)S(1)}, bf16[1,512,1024]{2,1,0:T(8,128)(2,1)}, u32[]{:S(2)}) copy-start(bf16[1,512,1024]{2,1,0:T(8,128)(2,1)} %param.18) | copy-start | bytes 3145732
  839.0 14.3 %copy-start.29 = (f32[512]{0:T(512)S(1)}, f32[512]{0:T(512)}, u32[]{:S(2)}) copy-start(f32[512]{0:T(512)} %copy-done.28) | copy-start | bytes 6148
  842.0 18.1 %copy-start.33 = (f32[512]{0:T(512)S(1)}, f32[512]{0:T(512)}, u32[]{:S(2)}) copy-start(f32[512]{0:T(512)} %copy-done.32) | copy-start | bytes 6148
  842.0 18.2 %copy-start.31 = (f32[512]{0:T(512)S(1)}, f32[512]{0:T(512)}, u32[]{:S(2)}) copy-start(f32[512]{0:T(512)} %copy-done.30) | copy-start | bytes 6148
  842.0 18.8 %copy-start.37 = (f32[512]{0:T(512)S(1)}, f32[512]{0:T(512)}, u32[]{:S(2)}) copy-start(f32[512]{0:T(512)} %copy-done.36) | copy-start | bytes 6148
  853.4 7.5 copy-start.13
  860.1 1.6 copy-start.7
  860.8 2.7 copy-start.8
Sparse Core Ops, SparseCore 0:
  10.2 101.7 all-gather.6
  120.4 32.6 all-gather.8
  155.3 34.5 all-gather.10
  191.8 49.3 all-gather.12
  243.2 123.4 all-gather.14
  368.6 123.1 all-gather.16
  542.1 154.2 all-reduce.3
  699.2 154.1 reduce-scatter.1
where the time goes:
time: 880 us; the launch traced here: 873 us
  waiting for transfers between devices  311 us (35%)
  matrix products  209 us (24%)
  blocking collectives  170 us (19%)
  local copies, waits for them, and re-layouts  86.3 us (10%)
  other arithmetic  75 us (9%)
  between operations  14.9 us (2%)
    psum x1, blocking collectives, shards(): lax.psum((local_grads[0], local_grads[1], local_grads[2], local_grads[3],...  170 us
    all_gather x1, waiting for transfers between devices, shards(): lax.all_gather(shrink_weight, 'dp', axis=0, tiled=True)  113 us
    all_gather x1, waiting for transfers between devices, shards(): lax.all_gather(attend_weight, 'dp', axis=0, tiled=True)  100 us
    dot_general x4, matrix products, key_block(): jnp.einsum('hqk,khd->qhd', exps.astype(jnp.bfloat16), value_piece.reshape...  41.1 us
    reduce_sum x4, other arithmetic, key_block(): new_sum = run_sum * factor + jnp.sum(exps, axis=2)  36.8 us
    all_gather x1, waiting for transfers between devices, shards(): lax.all_gather(expand_weight, 'dp', axis=0, tiled=True)  35 us
    dot_general x4, matrix products, key_block(): jnp.einsum('qhd,khd->hqk', queries, key_piece.reshape(piece_rows, head_co...  34.1 us
    all_gather x1, waiting for transfers between devices, shards(): value_piece = lax.all_gather(value_rows, 'seq', axis=0, tiled=True)  30.3 us
  transfers between devices with their start and end apart: 8, of which 6 were waited for; matrix products, arithmetic and copies ran while one was open for 34% of the time, Pallas kernels for 0%

commit v1 on v0

v1 whole, which is shorter than its diff:
```python
import functools

import jax
import jax.numpy as jnp
from jax import lax
from jax.experimental import pallas as pl
from jax.experimental.pallas import tpu as pltpu
from jax.sharding import PartitionSpec as P

PREFIX = 10
HEAD = 64
PAIR = 128
PREFIX_ROWS = 16
blocked = -1e30
norm_epsilon = 1e-05
highest = lax.Precision.HIGHEST
VT_ROWS = 80
f32, bf16 = jnp.float32, jnp.bfloat16

def dot(a, b, ca, cb):
    return lax.dot_general(a, b, (((ca,), (cb,)), ((), ())), preferred_element_type=f32)

def lane(shape):
    return lax.broadcasted_iota(jnp.int32, shape, len(shape) - 1)

def head_half(h, shape):
    l = lane(shape)
    return (l < HEAD) if h == 0 else (l >= HEAD)

def split3(v):
    hi = v.astype(bf16)
    r = v - hi.astype(f32)
    mid = r.astype(bf16)
    lo = (r - mid.astype(f32)).astype(bf16)
    return hi.astype(f32), mid.astype(f32), lo.astype(f32)

def fwd_body(bq, bk, q_ref, k_ref, v_ref, pk_ref, pv_ref, mq_ref, mk_ref, pm_ref,
             o_ref, stat_ref, ka, vt, pka, pvt, qh):
    i = pl.program_id(0)
    s_len = k_ref.shape[0]

    @pl.when(i == 0)
    def _():
        ka[:, :PAIR] = k_ref[...]
        ka[:, PAIR:] = mk_ref[...]
        pka[:, :PAIR] = pk_ref[...]
        pka[:, PAIR:] = pm_ref[...]
        ones = jnp.where(lax.broadcasted_iota(jnp.int32, (16, s_len), 0) == 0, 1.0, 0.0).astype(bf16)
        vtr = v_ref[...].T
        pvr = pv_ref[...].T
        for h in (0, 1):
            vt[h, :HEAD, :] = vtr[h * HEAD:(h + 1) * HEAD, :]
            vt[h, HEAD:, :] = ones
            pvt[h, :HEAD, :] = pvr[h * HEAD:(h + 1) * HEAD, :]
            pvt[h, HEAD:, :] = ones[:, :PREFIX_ROWS]

    q = q_ref[...] * bf16(0.125)
    for h in (0, 1):
        qh[h, :, :PAIR] = jnp.where(head_half(h, q.shape), q, bf16(0))
        qh[h, :, PAIR:] = mq_ref[...]
    state = []
    for h in (0, 1):
        s = dot(pka[...], qh[h], 1, 1)
        m = jnp.max(s, axis=0, keepdims=True)
        p = jnp.exp(s - m)
        state += [m, dot(pvt[h], p.astype(bf16), 1, 0)]

    def block(start, state, first, causal):
        out = []
        start = pl.multiple_of(start, bk)
        scores = [dot(ka[pl.ds(start, bk), :], qh[h, first:, :], 1, 1) for h in (0, 1)]
        for h in (0, 1):
            m, acc = state[2 * h], state[2 * h + 1]
            s = scores[h]
            if causal:
                ok = lax.broadcasted_iota(jnp.int32, s.shape, 0) <= lane(s.shape)
                s = jnp.where(ok, s, blocked)
            if first:
                keep_m, keep_acc = m[:, :first], acc[:, :first]
                m, acc = m[:, first:], acc[:, first:]
            new = jnp.maximum(m, jnp.max(s, axis=0, keepdims=True))
            p = jnp.exp(s - new)
            acc = acc * jnp.exp(m - new) + dot(vt[h, :, pl.ds(start, bk)], p.astype(bf16), 1, 0)
            if first:
                new, acc = jnp.concatenate([keep_m, new], axis=1), jnp.concatenate([keep_acc, acc], axis=1)
            out += [new, acc]
        return tuple(out)

    state = lax.fori_loop(
        0, i * (bq // bk), lambda j, st: block(j * bk, st, 0, False), tuple(state)
    )
    for jj in range(bq // bk):
        state = block(i * bq + jj * bk, state, jj * bk, True)
    outs, rows = [], []
    for h in (0, 1):
        m, acc = state[2 * h], state[2 * h + 1]
        total = acc[HEAD:HEAD + 1]
        outs.append(acc[:HEAD] / total)
        rows.append(-(m + jnp.log(total)))
    o_ref[...] = jnp.concatenate(outs, axis=0).T.astype(bf16)
    parts = [p for r in rows for p in split3(r)]
    pad = jnp.zeros((PAIR - 4 - len(parts), bq), f32)
    st = jnp.concatenate([jnp.zeros((4, bq), f32)] + parts + [pad], axis=0).T
    stat_ref[...] = (st + mq_ref[...].astype(f32)).astype(bf16)

def attn_fwd(qkv, pk, pv, mq, mk, pm):
    s_len = qkv.shape[0]
    bq, bk = min(2048, s_len), min(512, s_len)
    full = lambda c: pl.BlockSpec((s_len, PAIR), lambda i: (0, c))
    few = pl.BlockSpec((PREFIX_ROWS, PAIR), lambda i: (0, 0))
    row = pl.BlockSpec((bq, PAIR), lambda i: (i, 0))
    return pl.pallas_call(
        functools.partial(fwd_body, bq, bk),
        grid=(s_len // bq,),
        in_specs=[row, full(1), full(2), few, few, row, full(0), few],
        out_specs=[row, row],
        out_shape=[jax.ShapeDtypeStruct((s_len, PAIR), bf16)] * 2,
        scratch_shapes=[
            pltpu.VMEM((s_len, 2 * PAIR), bf16),
            pltpu.VMEM((2, VT_ROWS, s_len), bf16),
            pltpu.VMEM((PREFIX_ROWS, 2 * PAIR), bf16),
            pltpu.VMEM((2, VT_ROWS, PREFIX_ROWS), bf16),
            pltpu.VMEM((2, bq, 2 * PAIR), bf16),
        ],
        compiler_params=pltpu.CompilerParams(vmem_limit_bytes=48 << 20),
        cost_estimate=pl.CostEstimate(
            flops=2 * s_len * s_len * 512, bytes_accessed=s_len * PAIR * 16,
            transcendentals=s_len * s_len,
        ),
        name="attn_fwd",
    )(qkv, qkv, qkv, pk, pv, mq, mk, pm)


def bwd_body(bq, bk, q_ref, k_ref, v_ref, pk_ref, pv_ref, stat_ref, mk_ref, pm_ref, o_ref, do_ref,
             grad_ref, dp_ref, ka, va, kt, pka, pva, pkt, qh, dh, dk_acc, dv_acc, dpk_acc, dpv_acc):
    i = pl.program_id(0)
    s_len = k_ref.shape[0]

    @pl.when(i == 0)
    def _():
        ones = jnp.where(lane((s_len, PAIR)) < 3, 1.0, 0.0).astype(bf16)
        for h in (0, 1):
            l = lane((s_len, PAIR))
            mine = (l >= 4 + 3 * h) & (l < 7 + 3 * h)
            ka[h, :, :PAIR] = k_ref[...]
            ka[h, :, PAIR:] = jnp.where(mine, bf16(1), mk_ref[...])
            pka[h, :, :PAIR] = pk_ref[...]
            pka[h, :, PAIR:] = jnp.where(mine[:PREFIX_ROWS], bf16(1), pm_ref[...])
        va[:, :PAIR] = v_ref[...]
        va[:, PAIR:] = ones
        pva[:, :PAIR] = pv_ref[...]
        pva[:, PAIR:] = ones[:PREFIX_ROWS]
        kt[...] = k_ref[...].T
        pkt[...] = pk_ref[...].T
        dk_acc[...] = jnp.zeros_like(dk_acc)
        dv_acc[...] = jnp.zeros_like(dv_acc)
        dpk_acc[...] = jnp.zeros_like(dpk_acc)
        dpv_acc[...] = jnp.zeros_like(dpv_acc)

    q = q_ref[...] * bf16(0.125)
    do = do_ref[...]
    prod = do.astype(f32) * o_ref[...].astype(f32)
    for h in (0, 1):
        half = head_half(h, q.shape)
        qh[h, :, :PAIR] = jnp.where(half, q, bf16(0))
        qh[h, :, PAIR:] = stat_ref[...]
        dh[h, :, :PAIR] = jnp.where(half, do, bf16(0))
        delta = -jnp.sum(jnp.where(half, prod, 0.0), axis=1, keepdims=True)
        hi, mid, lo = split3(delta)
        l = lane((bq, PAIR))
        dh[h, :, PAIR:] = jnp.where(l == 0, hi, jnp.where(l == 1, mid, jnp.where(l == 2, lo, 0.0))).astype(bf16)

    dq_state = []
    for h in (0, 1):
        p = jnp.exp(dot(pka[h], qh[h], 1, 1))
        ds = (p * dot(pva[...], dh[h], 1, 1)).astype(bf16)
        dpv_acc[...] += dot(p.astype(bf16), dh[h, :, :PAIR], 1, 0)
        dpk_acc[...] += dot(ds, qh[h, :, :PAIR], 1, 0)
        dq_state.append(dot(pkt[h * HEAD:(h + 1) * HEAD, :], ds, 1, 0))

    def block(start, state, first, causal):
        start = pl.multiple_of(start, bk)
        at = pl.ds(start, bk)
        out = []
        dv = dk = None
        ss = [dot(ka[h, at, :], qh[h, first:, :], 1, 1) for h in (0, 1)]
        dps = [dot(va[at, :], dh[h, first:, :], 1, 1) for h in (0, 1)]
        for h in (0, 1):
            s = ss[h]
            p = jnp.exp(s)
            if causal:
                ok = lax.broadcasted_iota(jnp.int32, s.shape, 0) <= lane(s.shape)
                p = jnp.where(ok, p, 0.0)
            ds = (p * dps[h]).astype(bf16)
            a = dot(p.astype(bf16), dh[h, first:, :PAIR], 1, 0)
            b = dot(ds, qh[h, first:, :PAIR], 1, 0)
            dv = a if dv is None else dv + a
            dk = b if dk is None else dk + b
            c = dot(kt[h * HEAD:(h + 1) * HEAD, at], ds, 1, 0)
            if first:
                out.append(jnp.concatenate([state[h][:, :first], state[h][:, first:] + c], axis=1))
            else:
                out.append(state[h] + c)
        dv_acc[at, :] += dv
        dk_acc[at, :] += dk
        return tuple(out)

    state = lax.fori_loop(
        0, i * (bq // bk), lambda j, st: block(j * bk, st, 0, False), tuple(dq_state)
    )
    for jj in range(bq // bk):
        state = block(i * bq + jj * bk, state, jj * bk, True)
    grad_ref[pl.ds(pl.multiple_of(i * bq, bq), bq), :PAIR] = (
        (jnp.concatenate(state, axis=0) * 0.125).T.astype(bf16)
    )

    @pl.when(i == pl.num_programs(0) - 1)
    def _():
        grad_ref[:, PAIR : 2 * PAIR] = dk_acc[...].astype(bf16)
        grad_ref[:, 2 * PAIR :] = dv_acc[...].astype(bf16)
        dp_ref[0] = dpk_acc[...]
        dp_ref[1] = dpv_acc[...]

def attn_bwd(qkv, pk, pv, stat, mk, pm, o, do):
    s_len = qkv.shape[0]
    bq, bk = min(2048, s_len), min(256, s_len)
    full = lambda c: pl.BlockSpec((s_len, PAIR), lambda i: (0, c))
    few = pl.BlockSpec((PREFIX_ROWS, PAIR), lambda i: (0, 0))
    row = pl.BlockSpec((bq, PAIR), lambda i: (i, 0))
    return pl.pallas_call(
        functools.partial(bwd_body, bq, bk),
        grid=(s_len // bq,),
        in_specs=[row, full(1), full(2), few, few, row, full(0), few, row, row],
        out_specs=[
            pl.BlockSpec((s_len, 3 * PAIR), lambda i: (0, 0)),
            pl.BlockSpec((2, PREFIX_ROWS, PAIR), lambda i: (0, 0, 0)),
        ],
        out_shape=[
            jax.ShapeDtypeStruct((s_len, 3 * PAIR), bf16),
            jax.ShapeDtypeStruct((2, PREFIX_ROWS, PAIR), f32),
        ],
        scratch_shapes=[
            pltpu.VMEM((2, s_len, 2 * PAIR), bf16),
            pltpu.VMEM((s_len, 2 * PAIR), bf16),
            pltpu.VMEM((PAIR, s_len), bf16),
            pltpu.VMEM((2, PREFIX_ROWS, 2 * PAIR), bf16),
            pltpu.VMEM((PREFIX_ROWS, 2 * PAIR), bf16),
            pltpu.VMEM((PAIR, PREFIX_ROWS), bf16),
            pltpu.VMEM((2, bq, 2 * PAIR), bf16),
            pltpu.VMEM((2, bq, 2 * PAIR), bf16),
            pltpu.VMEM((s_len, PAIR), f32),
            pltpu.VMEM((s_len, PAIR), f32),
            pltpu.VMEM((PREFIX_ROWS, PAIR), f32),
            pltpu.VMEM((PREFIX_ROWS, PAIR), f32),
        ],
        compiler_params=pltpu.CompilerParams(vmem_limit_bytes=48 << 20),
        cost_estimate=pl.CostEstimate(
            flops=5 * s_len * s_len * 512, bytes_accessed=s_len * PAIR * 24,
            transcendentals=s_len * s_len,
        ),
        name="attn_bwd",
    )(qkv, qkv, qkv, pk, pv, stat, mk, pm, o, do)


def masks(lengths, s_len):
    e0 = lengths[0]; e1 = e0 + lengths[1]; e2 = e1 + lengths[2]
    pos = jnp.arange(s_len, dtype=jnp.int32)
    doc = sum((pos >= e).astype(jnp.int32) for e in (e0, e1, e2))
    l = lax.broadcasted_iota(jnp.int32, (s_len, PAIR), 1)
    same = l == doc[:, None]
    mq = jnp.where((l < 4) & ~same, blocked, 0.0).astype(bf16)
    mk = jnp.where((l < 4) & same, 1.0, 0.0).astype(bf16)
    r = lax.broadcasted_iota(jnp.int32, (PREFIX_ROWS, PAIR), 0)
    lp = lax.broadcasted_iota(jnp.int32, (PREFIX_ROWS, PAIR), 1)
    pm = jnp.where((r >= PREFIX) & (lp == 3), 1.0, 0.0).astype(bf16)
    return mq, mk, pm


def layer_norm(hidden):
    centered = hidden - jnp.mean(hidden, axis=-1, keepdims=True)
    return centered * lax.rsqrt(
        jnp.mean(centered * centered, axis=-1, keepdims=True) + norm_epsilon
    )


def gelu_tanh(values):
    return (
        0.5
        * values
        * (1.0 + jnp.tanh(0.7978845608028654 * (values + 0.044715 * values * values * values)))
    )


def reparam(embedding, inner_matrix, inner_shift, outer_matrix, outer_shift):
    hidden = jnp.tanh(
        jnp.dot(embedding, inner_matrix, precision=highest, preferred_element_type=f32)
        + inner_shift
    )
    return (
        jnp.dot(hidden, outer_matrix, precision=highest, preferred_element_type=f32) + outer_shift
    )


def halvings(count):
    steps = []
    while count > 1:
        count //= 2
        steps.append(count)
    return steps


def swap(value, axis, size, mask):
    return lax.ppermute(value, axis, [(i, i ^ mask) for i in range(size)])


def put(buffer, piece, starts):
    return lax.dynamic_update_slice(buffer, piece, starts)


def gather_dp(piece, dp):
    me = lax.axis_index("dp")
    near = 2 if dp % 2 == 0 else 1
    far = dp // near
    mine = me // near
    zero = (0,) * piece.ndim
    line = put(jnp.zeros((far,) + piece.shape, piece.dtype), piece[None], (mine,) + zero)
    for k in range(1, far):
        got = lax.ppermute(piece, "dp", [(i, (i + near * k) % dp) for i in range(dp)])
        line = put(line, got[None], (lax.rem(mine - k + far, far),) + zero)
    if near == 1:
        return line
    other = swap(line, "dp", dp, 1)
    side = lax.rem(me, 2)
    both = jnp.zeros((far, 2) + piece.shape, piece.dtype)
    both = put(both, line[:, None], (0, side) + zero)
    both = put(both, other[:, None], (0, 1 - side) + zero)
    return both.reshape((dp,) + piece.shape)


def spread_seq(value, seq):
    held = {0: value}
    for mask in halvings(seq):
        for r in list(held):
            held[r ^ mask] = swap(held[r], "seq", seq, mask)
    return [held[r] for r in range(seq)]


def exchange_seq(pieces, seq):
    return [pieces[0]] + [swap(pieces[r], "seq", seq, r) for r in range(1, seq)]


def shards(seq, dp, tokens, lengths, attend_weight, output_weight, expand_weight, shrink_weight,
           prefix_embed, inner_weight, inner_bias, outer_weight, outer_bias, cotangent):
    s = lax.axis_index("seq")
    rows, width = tokens.shape[1:]
    s_len = rows * seq
    cols = width // seq
    pairs = cols // PAIR
    token_rows = tokens[0].astype(f32)
    upstream = cotangent[0]

    normed_full, input_norm_back = jax.vjp(layer_norm, token_rows)
    normed_all = jnp.zeros((s_len, width), bf16)
    for r, got in enumerate(spread_seq(normed_full.astype(bf16), seq)):
        normed_all = put(normed_all, got, ((s ^ r) * rows, 0))

    shard_rows = attend_weight.shape[0]
    parts = attend_weight.reshape(shard_rows, 3, seq, pairs, PAIR)
    mine = lax.dynamic_index_in_dim(parts, s, 2, keepdims=False)
    attend_pairs = [
        gather_dp(mine[:, :, p].reshape(shard_rows, 3 * PAIR), dp).reshape(width, 3 * PAIR)
        for p in range(pairs)
    ]
    quarter = output_weight.shape[0] // seq
    got = spread_seq(
        gather_dp(lax.dynamic_slice_in_dim(output_weight, s * quarter, quarter, 0), dp), seq
    )
    full_output = jnp.zeros((dp, seq, quarter, width), bf16)
    for r in range(seq):
        full_output = put(full_output, got[r][:, None], (0, s ^ r, 0, 0))
    full_output = full_output.reshape(width, width)
    hidden = expand_weight.shape[1]
    chunk = hidden // dp // seq
    piece = lax.dynamic_index_in_dim(
        expand_weight.reshape(shard_rows, dp, seq, chunk), s, 2, keepdims=False
    ).reshape(shard_rows, dp * chunk)
    expand_parts = [w.reshape(width, dp * chunk) for w in spread_seq(gather_dp(piece, dp), seq)]
    piece = lax.dynamic_slice_in_dim(shrink_weight, s * chunk, chunk, 0)
    shrink_parts = [w.reshape(dp * chunk, width) for w in spread_seq(gather_dp(piece, dp), seq)]

    prefix_kv, reparam_back = jax.vjp(
        reparam, prefix_embed, inner_weight, inner_bias, outer_weight, outer_bias
    )
    padded = jnp.pad(prefix_kv.astype(bf16), ((0, PREFIX_ROWS - PREFIX), (0, 0)))
    prefix_mine = lax.dynamic_index_in_dim(
        padded.reshape(PREFIX_ROWS, 2, seq, pairs, PAIR), s, 2, keepdims=False
    )
    mask_q, mask_k, mask_p = masks(lengths[0], s_len)

    qkv, attended, stats, own_heads = [], [], [], []
    for p in range(pairs):
        projected = jnp.dot(normed_all, attend_pairs[p], preferred_element_type=f32).astype(bf16)
        out, stat = attn_fwd(projected, prefix_mine[:, 0, p], prefix_mine[:, 1, p], mask_q, mask_k, mask_p)
        qkv.append(projected)
        attended.append(out)
        stats.append(stat)
        own_heads.append(
            exchange_seq(
                [lax.dynamic_slice_in_dim(out, (s ^ r) * rows, rows, 0) for r in range(seq)], seq
            )
        )
    merged = jnp.zeros((rows, width), bf16)
    for p in range(pairs):
        for r in range(seq):
            merged = put(merged, own_heads[p][r], (0, (s ^ r) * cols + p * PAIR))
    residual_mid = token_rows + jnp.dot(merged, full_output, preferred_element_type=f32)
    normed_mid, mid_norm_back = jax.vjp(layer_norm, residual_mid)
    normed_mid = normed_mid.astype(bf16)
    outputs = residual_mid
    normed_grad = jnp.zeros((rows, width), f32)
    for up, down in zip(expand_parts, shrink_parts):
        expanded = jnp.dot(normed_mid, up, preferred_element_type=f32)
        activated, gelu_back = jax.vjp(gelu_tanh, expanded)
        outputs = outputs + jnp.dot(activated.astype(bf16), down, preferred_element_type=f32)
        expand_grad = gelu_back(dot(upstream, down, 1, 1))[0].astype(bf16)
        normed_grad = normed_grad + dot(expand_grad, up, 1, 1)
    mid_grad = upstream.astype(f32) + mid_norm_back(normed_grad)[0]
    out_grad = dot(mid_grad.astype(bf16), full_output, 1, 1).astype(bf16)

    partial = jnp.zeros((s_len, width), f32)
    prefix_terms = []
    for p in range(pairs):
        sent = [
            lax.dynamic_slice(out_grad, (0, (s ^ r) * cols + p * PAIR), (rows, PAIR))
            for r in range(seq)
        ]
        out_all = jnp.zeros((s_len, PAIR), bf16)
        for r, got in enumerate(exchange_seq(sent, seq)):
            out_all = put(out_all, got, ((s ^ r) * rows, 0))
        grads, prefix_part = attn_bwd(
            qkv[p], prefix_mine[:, 0, p], prefix_mine[:, 1, p], stats[p], mask_k, mask_p,
            attended[p], out_all,
        )
        partial = partial + dot(grads, attend_pairs[p], 1, 1)
        prefix_terms.append(prefix_part)

    blocks = {r: lax.dynamic_slice_in_dim(partial, (s ^ r) * rows, rows, 0) for r in range(seq)}
    for mask in reversed(halvings(seq)):
        keep = {r: blocks[r] for r in blocks if not r & mask}
        for r in keep:
            got = swap(blocks[r ^ mask].astype(bf16), "seq", seq, mask)
            keep[r] = blocks[r] + got.astype(f32)
        blocks = keep
    input_grad = mid_grad + input_norm_back(blocks[0])[0]

    prefix_sum = jnp.stack(prefix_terms, axis=2)
    for mask in halvings(dp):
        prefix_sum = prefix_sum + swap(prefix_sum, "dp", dp, mask)
    prefix_grad = jnp.zeros((2, PREFIX_ROWS, seq, pairs, PAIR), f32)
    for r, got in enumerate(spread_seq(prefix_sum, seq)):
        prefix_grad = put(prefix_grad, got[:, :, None], (0, 0, s ^ r, 0, 0))
    prefix_grad = prefix_grad[:, :PREFIX].reshape(2, PREFIX, width)
    back = reparam_back(jnp.concatenate([prefix_grad[0], prefix_grad[1]], axis=1))
    return (outputs.astype(bf16)[None], input_grad.astype(bf16)[None], *back, prefix_kv)


def solution(mesh):
    placed = (
        P("dp", "seq", None),
        P("dp", None),
        P("dp", None),
        P("dp", None),
        P("dp", None),
        P("dp", None),
        P(),
        P(),
        P(),
        P(),
        P(),
        P("dp", "seq", None),
    )
    return jax.shard_map(
        functools.partial(shards, mesh.shape["seq"], mesh.shape["dp"]),
        mesh=mesh,
        in_specs=placed,
        out_specs=(P("dp", "seq", None), P("dp", "seq", None), P(), P(), P(), P(), P(), P()),
        check_vma=False,
    )
```

time: 880 us -> 456 us (0.52)
  waiting for transfers between devices: 311 us -> 107 us
  blocking collectives: 170 us -> 0 us
  matrix products: 209 us -> 105 us
  starting transfers between devices: 0.31 us -> 69.7 us
  other arithmetic: 75 us -> 19.1 us
  Pallas kernels: 0 us -> 46.5 us
  between operations: 14.9 us -> 4.13 us
    all_gather x6 -> x0, waiting for transfers between devices: 296 us -> none  [the longest x1 113 us: shards(): lax.all_gather(shrink_weight, 'dp', axis=0, tiled=True)]
    psum x1 -> x0, blocking collectives: 170 us -> none  [shards(): lax.psum((local_grads[0], local_grads[1], local_grads[2], local_grads[3],...]
    ppermute x0 -> x53, waiting for transfers between devices: none -> 107 us  [the longest x38 104 us: swap(): return lax.ppermute(value, axis, [(i, i ^ mask) for i in range(size)])]
    dot_general x29 -> x21, matrix products: 203 us -> 98.3 us  [the longest x7 42.5 us: dot(): lax.dot_general(a, b, (((ca,), (cb,)), ((), ())), preferred_element_type=...]
    ppermute x0 -> x53, starting transfers between devices: none -> 69.7 us  [the longest x38 44.4 us: swap(): return lax.ppermute(value, axis, [(i, i ^ mask) for i in range(size)])]
    pallas_call x0 -> x4, Pallas kernels: none -> 46.5 us  [the longest x2 30.5 us: attn_bwd(): pl.pallas_call(functools.partial(bwd_body, bq, bk), grid=(s_len // bq,),...]
    reduce_sum x13 -> x2, other arithmetic: 39.8 us -> 3.22 us  [the longest x1 2.59 us: layer_norm(): centered * lax.rsqrt(jnp.mean(centered * centered, axis=-1, keepdims=True...]
    dynamic_update_slice x8 -> x53, local copies, waits for them, and re-layouts: 28.5 us -> 47.3 us  [put(): return lax.dynamic_update_slice(buffer, piece, starts)]
  transfers between devices with their start and end apart: 8 -> 53, of which waited for: 6 -> 17; matrix products, arithmetic and copies ran while one was open for 34% -> 42% of each run, Pallas kernels for 0% -> 4%
where the time goes in v1:
time: 456 us; the launch traced here: 447 us
  waiting for transfers between devices  107 us (23%)
  matrix products  105 us (23%)
  local copies, waits for them, and re-layouts  95.1 us (21%)
  starting transfers between devices  69.7 us (15%)
  Pallas kernels  46.5 us (10%)
  other arithmetic  19.1 us (4%)
    ppermute x38, waiting for transfers between devices, swap(): return lax.ppermute(value, axis, [(i, i ^ mask) for i in range(size)])  104 us
    dynamic_update_slice x53, local copies, waits for them, and re-layouts, put(): return lax.dynamic_update_slice(buffer, piece, starts)  47.3 us
    ppermute x38, starting transfers between devices, swap(): return lax.ppermute(value, axis, [(i, i ^ mask) for i in range(size)])  44.4 us
    dot_general x7, matrix products, dot(): lax.dot_general(a, b, (((ca,), (cb,)), ((), ())), preferred_element_type=...  42.5 us
    pallas_call x2, Pallas kernels, attn_bwd(): pl.pallas_call(functools.partial(bwd_body, bq, bk), grid=(s_len // bq,),...  30.5 us
    ppermute x15, starting transfers between devices, gather_dp(): lax.ppermute(piece, 'dp', [(i, (i + near * k) % dp) for i in range(dp)])  25.3 us
    dot_general x4, matrix products, shards(): jnp.dot(activated.astype(bf16), down, preferred_element_type=f32)  17.9 us
    pallas_call x2, Pallas kernels, attn_fwd(): pl.pallas_call(functools.partial(fwd_body, bq, bk), grid=(s_len // bq,),...  16 us
  transfers between devices with their start and end apart: 53, of which 17 were waited for; matrix products, arithmetic and copies ran while one was open for 42% of the time, Pallas kernels for 4%

profile of v1, /device:TPU:0, one launch (start us, length us, event | category | flops | bytes accessed | tf_op | source)
XLA Modules:
  0.0 446.7 jit_solution(17615538331311618186)
XLA Ops:
  3.0 4.0 collective-permute-start.18
  8.6 2.2 collective-permute-start.19
  10.8 3.2 reshape.141
  14.1 1.8 constant_dynamic-slice_fusion.16
  18.4 2.0 collective-permute-start.10
  25.9 4.9 %fusion.142 = (bf16[10,2048]{1,0:T(8,128)(2,1)S(1)}, f32[10,2048]{1,0:T(8,128)}) fusion(f32[2048]{0:T(1024)S(1)} %copy-done.42, f32[10,512]{1,0:T(8,128)S(1)} %fusion.50, f32[512,2048]{1,0:T(8,128)} %param.21), kind=kOutput, calls=%fused_computation.289 | convolution fusion | flops 125870080 | bytes 4345856 | tf_op jit(solution)/shard_map/jvp()/dot_general | solution.py:300
  41.0 1.8 bitcast_dynamic-update-slice_fusion.15
  45.3 2.0 copy-done.25
  48.9 1.8 collective-permute-start.5
  56.5 1.7 bitcast_dynamic-update-slice_fusion.11
  58.2 2.6 collective-permute-start.11
  62.4 2.7 collective-permute-start.26
  72.0 2.4 collective-permute-start.29
  77.6 4.6 %collective-permute-start.28 = (bf16[128,1024]{1,0:T(8,128)(2,1)}, bf16[128,1024]{1,0:T(8,128)(2,1)}, u32[]{:S(2)}, u32[]{:S(2)}) collective-permute-start(bf16[128,1024]{1,0:T(8,128)(2,1)} %get-tuple-element.57), channel_id=1, source_target_pairs={{0,2},{1,3},{2,4},{3,5},{4,6},{5,7},{6,0},{7,1},{8,10},{9,11},{10,... | collective-permute-start | bytes 786440 | tf_op jit(solution)/shard_map/ppermute | solution.py:328
  84.7 1.8 bitcast_dynamic-update-slice_fusion.8
  88.1 1.8 bitcast_dynamic-update-slice_fusion.9
  90.8 1.8 copy.82
  94.2 1.7 bitcast_dynamic-update-slice_fusion.14
  95.8 1.7 constant_dynamic-update-slice_fusion.8
  99.0 1.8 copy.84
  104.4 1.7 constant_dynamic-update-slice_fusion.6
  108.1 1.7 bitcast_dynamic-update-slice_fusion.13
  115.1 2.4 bitcast_dynamic-update-slice_fusion.1
  120.2 1.7 bitcast_dynamic-update-slice_fusion.16
  129.5 6.2 %collective-permute-done.22 = bf16[8,32,1024]{2,1,0:T(8,128)(2,1)S(1)} collective-permute-done((bf16[8,32,1024]{2,1,0:T(8,128)(2,1)}, bf16[8,32,1024]{2,1,0:T(8,128)(2,1)S(1)}, u32[]{:S(2)}, u32[]{:S(2)}) %collective-permute-start.22) | collective-permute-done | bytes 524320 | tf_op jit(solution)/shard_map/ppermute | solution.py:313
  139.5 12.9 %collective-permute-done.27 = bf16[4,128,1024]{2,1,0:T(8,128)(2,1)S(1)} collective-permute-done((bf16[4,128,1024]{2,1,0:T(8,128)(2,1)S(1)}, bf16[4,128,1024]{2,1,0:T(8,128)(2,1)S(1)}, u32[]{:S(2)}, u32[]{:S(2)}) %collective-permute-start.27) | collective-permute-done | bytes 1048608 | tf_op jit(solution)/shard_map/ppermute | solution.py:313
  154.0 19.1 %collective-permute-done.31 = bf16[4,128,1024]{2,1,0:T(8,128)(2,1)S(1)} collective-permute-done((bf16[4,128,1024]{2,1,0:T(8,128)(2,1)}, bf16[4,128,1024]{2,1,0:T(8,128)(2,1)S(1)}, u32[]{:S(2)}, u32[]{:S(2)}) %collective-permute-start.31) | collective-permute-done | bytes 1048608 | tf_op jit(solution)/shard_map/ppermute | solution.py:313
  174.3 3.5 convolution_convert_fusion.q_ref.k_ref.v_ref
  177.7 4.0 convolution_convert_fusion.1.q_ref.k_ref.v_ref
  181.8 8.2 %attn_fwd.2 = (bf16[2048,128]{1,0:T(8,128)(2,1)S(1)}, bf16[2048,128]{1,0:T(8,128)(2,1)S(1)}) custom-call(bf16[2048,384]{1,0:T(8,128)(2,1)S(1)} %convolution_convert_fusion.1.q_ref.k_ref.v_ref, bf16[2048,384]{1,0:T(8,128)(2,1)S(1)} %convolution_convert_fusion.1.q_ref.k_ref.v_ref, bf16[2048,384]{1,0:T(8,128)(2,1)S(1)} %convolution_convert_fusion.1.q_ref.k_ref.v_ref, ...), custom_call_target="tpu_custom_call" | custom-call | flops 4294967296 | bytes 4194304 | tf_op jit(solution)/shard_map/attn_fwd/pallas_call | solution.py:112
  191.5 7.8 %attn_fwd.3 = (bf16[2048,128]{1,0:T(8,128)(2,1)S(1)}, bf16[2048,128]{1,0:T(8,128)(2,1)S(1)}) custom-call(bf16[2048,384]{1,0:T(8,128)(2,1)S(1)} %convolution_convert_fusion.q_ref.k_ref.v_ref, bf16[2048,384]{1,0:T(8,128)(2,1)S(1)} %convolution_convert_fusion.q_ref.k_ref.v_ref, bf16[2048,384]{1,0:T(8,128)(2,1)S(1)} %convolution_convert_fusion.q_ref.k_ref.v_ref, ...), custom_call_target="tpu_custom_call" | custom-call | flops 4294967296 | bytes 4194304 | tf_op jit(solution)/shard_map/attn_fwd/pallas_call | solution.py:112
  199.3 1.7 collective-permute-start.9
  201.7 3.2 collective-permute-done.9
  208.6 45.0 %collective-permute-done.15 = bf16[512,128]{1,0:T(8,128)(2,1)S(1)} collective-permute-done((bf16[512,128]{1,0:T(8,128)(2,1)S(1)}, bf16[512,128]{1,0:T(8,128)(2,1)S(1)}, u32[]{:S(2)}, u32[]{:S(2)}) %collective-permute-start.15) | collective-permute-done | bytes 131104 | tf_op jit(solution)/shard_map/ppermute | solution.py:313
  257.9 3.4 fusion.147
  262.6 4.3 fusion.52
  266.9 7.8 %fusion.49 = f32[512,1024]{1,0:T(8,128)} fusion(bf16[1024,1024]{1,0:T(8,128)(2,1)} %bitcast.55, f32[512,1024]{1,0:T(8,128)} %copy-done.47, bf16[1024,1024]{1,0:T(8,128)(2,1)} %bitcast.64, bf16[1,512,1024]{2,1,0:T(8,128)(2,1)} %param.23), kind=kOutput, calls=%fused_computation.98 | convolution fusion | flops 2160066560 | bytes 9437184 | tf_op jit(solution)/shard_map/dot_general | solution.py:21
  275.2 3.2 fusion.149
  278.5 3.6 fusion.148
  282.1 5.1 %fusion.54 = f32[512,1024]{1,0:T(8,128)} fusion(bf16[1024,1024]{1,0:T(8,128)(2,1)} %bitcast.70, f32[512,1024]{1,0:T(8,128)S(1)} %fusion.149), kind=kOutput, calls=%fused_computation.104 | convolution fusion | flops 1078460416 | bytes 6291456 | tf_op jit(solution)/shard_map/dot_general | solution.py:424
  287.2 4.3 fusion.53
  291.6 7.9 %fusion.47 = f32[512,1024]{1,0:T(8,128)} fusion(bf16[1024,1024]{1,0:T(8,128)(2,1)} %bitcast.69, f32[512,1024]{1,0:T(8,128)} %copy-done.45, bf16[1024,1024]{1,0:T(8,128)(2,1)} %bitcast.70, bf16[1,512,1024]{2,1,0:T(8,128)(2,1)} %param.23), kind=kOutput, calls=%fused_computation.96 | convolution fusion | flops 2160066560 | bytes 9437184 | tf_op jit(solution)/shard_map/dot_general | solution.py:21
  299.4 8.0 %fusion.48 = f32[512,1024]{1,0:T(8,128)} fusion(bf16[1024,1024]{1,0:T(8,128)(2,1)} %bitcast.66, f32[512,1024]{1,0:T(8,128)} %copy-done.46, bf16[1024,1024]{1,0:T(8,128)(2,1)} %bitcast.68, bf16[1,512,1024]{2,1,0:T(8,128)(2,1)} %param.23), kind=kOutput, calls=%fused_computation.97 | convolution fusion | flops 2160066560 | bytes 9437184 | tf_op jit(solution)/shard_map/dot_general | solution.py:21
  307.4 4.5 fusion.150
  311.9 10.5 %multiply_reduce_fusion = (f32[512]{0:T(512)S(1)}, f32[512,1024]{1,0:T(8,128)}) fusion(f32[512,1024]{1,0:T(8,128)} %copy-done.14, f32[512]{0:T(512)S(1)} %broadcast_multiply_fusion, bf16[1024,1024]{1,0:T(8,128)(2,1)} %bitcast.71, f32[512,1024]{1,0:T(8,128)} %fusion.150, bf16[1024,1024]{1,0:T(8,128)(2,1)} %bitcast.72, bf16[1,512,1024]{2,1,0:T(8,128)(2,1)} %param.23, ...), kind=kOutput, calls=%fused_computation.83 | convolution fusion | flops 2163211776 | bytes 17829888 | tf_op jit(solution)/shard_map/dot_general | solution.py:21
  322.4 3.0 fusion.137
  331.3 4.2 fusion.45
  335.7 3.6 collective-permute-done.42
  339.3 2.2 collective-permute-done.39
  341.7 15.5 %attn_bwd.2 = (bf16[2048,384]{1,0:T(8,128)(2,1)S(1)}, f32[2,16,128]{2,1,0:T(8,128)S(1)}) custom-call(bf16[2048,384]{1,0:T(8,128)(2,1)S(1)} %copy-done.8, bf16[2048,384]{1,0:T(8,128)(2,1)S(1)} %copy-done.8, bf16[2048,384]{1,0:T(8,128)(2,1)S(1)} %copy-done.8, bf16[16,128]{1,0:T(8,128)(2,1)S(1)} %get-tuple-element.82.pk_ref, ...), custom_call_target="tpu_custom_call" | custom-call | flops 10737418240 | bytes 6291456 | tf_op jit(solution)/shard_map/attn_bwd/pallas_call | solution.py:230
  357.2 15.1 %attn_bwd.3 = (bf16[2048,384]{1,0:T(8,128)(2,1)S(1)}, f32[2,16,128]{2,1,0:T(8,128)S(1)}) custom-call(bf16[2048,384]{1,0:T(8,128)(2,1)S(1)} %copy-done.6, bf16[2048,384]{1,0:T(8,128)(2,1)S(1)} %copy-done.6, bf16[2048,384]{1,0:T(8,128)(2,1)S(1)} %copy-done.6, bf16[16,128]{1,0:T(8,128)(2,1)S(1)} %get-tuple-element.80.pk_ref, ...), custom_call_target="tpu_custom_call" | custom-call | flops 10737418240 | bytes 6291456 | tf_op jit(solution)/shard_map/attn_bwd/pallas_call | solution.py:230
  372.3 18.5 %collective-permute-start.47 = (f32[2,16,2,128]{3,1,0,2:T(8,128)S(1)}, f32[2,16,2,128]{3,1,0,2:T(8,128)S(1)}, u32[]{:S(2)}, u32[]{:S(2)}) collective-permute-start(f32[2,16,2,128]{3,1,0,2:T(8,128)S(1)} %pad_maximum_fusion), channel_id=1, source_target_pairs={{0,4},{1,5},{2,6},{3,7},{4,0},{5,1},{6,2},{7,3},{8,12},{9,13},{10,... | collective-permute-start | bytes 98312 | tf_op jit(solution)/shard_map/ppermute | solution.py:313
  390.7 3.5 fusion.151
  394.4 3.6 convolution_add_fusion
  405.1 2.3 collective-permute-done.51
  410.2 3.4 add_convert_fusion.1
  415.1 4.4 fusion.146
  420.2 3.2 convolution_bitcast_fusion
  423.3 2.9 copy.98
  426.2 2.5 fusion.152
  428.7 5.0 %fusion.153 = f32[512,2048]{1,0:T(8,128)} fusion(f32[10,512]{1,0:T(8,128)S(1)} %fusion.50, f32[10,2048]{1,0:T(8,128)S(1)} %constant_dynamic-update-slice_fusion.26), kind=kOutput, calls=%fused_computation.298 | convolution fusion | flops 125829120 | bytes 4296704 | tf_op jit(solution)/shard_map/transpose(jvp())/dot_general | solution.py:300
  433.7 5.5 %collective-permute-done.46 = bf16[512,1024]{1,0:T(8,128)(2,1)} collective-permute-done((bf16[512,1024]{1,0:T(8,128)(2,1)}, bf16[512,1024]{1,0:T(8,128)(2,1)}, u32[]{:S(2)}, u32[]{:S(2)}) %collective-permute-start.46) | collective-permute-done | bytes 1048608 | tf_op jit(solution)/shard_map/ppermute | solution.py:313
  439.2 2.6 fusion.8
  441.8 3.0 fusion.136
  (296 shorter events, 109.0 us)
Async XLA Ops:
  0.6 24.2 %copy-start = (f32[1024,512]{1,0:T(8,128)S(1)}, f32[1024,512]{1,0:T(8,128)}, u32[]{:S(2)}) copy-start(f32[1024,512]{1,0:T(8,128)} %param.19) | copy-start | bytes 6291460
  0.6 20.3 %copy-start.43 = (s32[1,3]{1,0:T(1,128)S(1)}, s32[1,3]{1,0:T(1,128)}, u32[]{:S(2)}) copy-start(s32[1,3]{1,0:T(1,128)} %param.13) | copy-start | bytes 40
  0.7 20.9 %copy-start.16 = (bf16[1,512,1024]{2,1,0:T(8,128)(2,1)S(1)}, bf16[1,512,1024]{2,1,0:T(8,128)(2,1)}, u32[]{:S(2)}) copy-start(bf16[1,512,1024]{2,1,0:T(8,128)(2,1)} %param.12) | copy-start | bytes 3145732
  3.0 49.1 %collective-permute-start.18 = (bf16[32,1024]{1,0:T(8,128)(2,1)}, bf16[32,1024]{1,0:T(8,128)(2,1)}, u32[]{:S(2)}, u32[]{:S(2)}) collective-permute-start(bf16[32,1024]{1,0:T(8,128)(2,1)} %get-tuple-element.53), channel_id=1, source_target_pairs={{0,4},{1,5},{2,6},{3,7},{4,0},{5,1},{6,2},{7,3},{8,12},{9,13},{10,... | collective-permute-start | bytes 196616 | tf_op jit(solution)/shard_map/ppermute | solution.py:328
  7.0 41.8 %collective-permute-start.17 = (bf16[32,1024]{1,0:T(8,128)(2,1)}, bf16[32,1024]{1,0:T(8,128)(2,1)}, u32[]{:S(2)}, u32[]{:S(2)}) collective-permute-start(bf16[32,1024]{1,0:T(8,128)(2,1)} %get-tuple-element.53), channel_id=1, source_target_pairs={{0,2},{1,3},{2,4},{3,5},{4,6},{5,7},{6,0},{7,1},{8,10},{9,11},{10,... | collective-permute-start | bytes 196616 | tf_op jit(solution)/shard_map/ppermute | solution.py:328
  8.6 45.0 %collective-permute-start.19 = (bf16[32,1024]{1,0:T(8,128)(2,1)}, bf16[32,1024]{1,0:T(8,128)(2,1)}, u32[]{:S(2)}, u32[]{:S(2)}) collective-permute-start(bf16[32,1024]{1,0:T(8,128)(2,1)} %get-tuple-element.53), channel_id=1, source_target_pairs={{0,6},{1,7},{2,0},{3,1},{4,2},{5,3},{6,4},{7,5},{8,14},{9,15},{10,... | collective-permute-start | bytes 196616 | tf_op jit(solution)/shard_map/ppermute | solution.py:328
  18.4 59.2 %collective-permute-start.12 = (bf16[128,384]{1,0:T(8,128)(2,1)}, bf16[128,384]{1,0:T(8,128)(2,1)}, u32[]{:S(2)}, u32[]{:S(2)}) collective-permute-start(bf16[128,384]{1,0:T(8,128)(2,1)} %copy.70), channel_id=1, source_target_pairs={{0,6},{1,7},{2,0},{3,1},{4,2},{5,3},{6,4},{7,5},{8,14},{9,15},{10,... | collective-permute-start | bytes 294920 | tf_op jit(solution)/shard_map/ppermute | solution.py:328
  18.4 50.0 %collective-permute-start.10 = (bf16[128,384]{1,0:T(8,128)(2,1)}, bf16[128,384]{1,0:T(8,128)(2,1)}, u32[]{:S(2)}, u32[]{:S(2)}) collective-permute-start(bf16[128,384]{1,0:T(8,128)(2,1)} %copy.70), channel_id=1, source_target_pairs={{0,2},{1,3},{2,4},{3,5},{4,6},{5,7},{6,0},{7,1},{8,10},{9,11},{10,... | collective-permute-start | bytes 294920 | tf_op jit(solution)/shard_map/ppermute | solution.py:328
  48.9 9.3 %collective-permute-start.5 = (bf16[128,384]{0,1:T(8,128)(2,1)}, bf16[128,384]{0,1:T(8,128)(2,1)}, u32[]{:S(2)}, u32[]{:S(2)}) collective-permute-start(bf16[128,384]{0,1:T(8,128)(2,1)} %bitcast.3), channel_id=1, source_target_pairs={{0,6},{1,7},{2,0},{3,1},{4,2},{5,3},{6,4},{7,5},{8,14},{9,15},{10,... | collective-permute-start | bytes 294920 | tf_op jit(solution)/shard_map/ppermute | solution.py:328
  52.1 10.3 %collective-permute-start.4 = (bf16[128,384]{0,1:T(8,128)(2,1)}, bf16[128,384]{0,1:T(8,128)(2,1)}, u32[]{:S(2)}, u32[]{:S(2)}) collective-permute-start(bf16[128,384]{0,1:T(8,128)(2,1)} %bitcast.3), channel_id=1, source_target_pairs={{0,4},{1,5},{2,6},{3,7},{4,0},{5,1},{6,2},{7,3},{8,12},{9,13},{10,... | collective-permute-start | bytes 294920 | tf_op jit(solution)/shard_map/ppermute | solution.py:328
  53.6 13.1 %collective-permute-start.3 = (bf16[128,384]{0,1:T(8,128)(2,1)}, bf16[128,384]{0,1:T(8,128)(2,1)}, u32[]{:S(2)}, u32[]{:S(2)}) collective-permute-start(bf16[128,384]{0,1:T(8,128)(2,1)} %bitcast.3), channel_id=1, source_target_pairs={{0,2},{1,3},{2,4},{3,5},{4,6},{5,7},{6,0},{7,1},{8,10},{9,11},{10,... | collective-permute-start | bytes 294920 | tf_op jit(solution)/shard_map/ppermute | solution.py:328
  58.2 13.9 %collective-permute-start.11 = (bf16[128,384]{1,0:T(8,128)(2,1)}, bf16[128,384]{1,0:T(8,128)(2,1)}, u32[]{:S(2)}, u32[]{:S(2)}) collective-permute-start(bf16[128,384]{1,0:T(8,128)(2,1)} %copy.70), channel_id=1, source_target_pairs={{0,4},{1,5},{2,6},{3,7},{4,0},{5,1},{6,2},{7,3},{8,12},{9,13},{10,... | collective-permute-start | bytes 294920 | tf_op jit(solution)/shard_map/ppermute | solution.py:328
  62.4 35.1 %collective-permute-start.26 = (bf16[128,1024]{0,1:T(8,128)(2,1)S(1)}, bf16[128,1024]{0,1:T(8,128)(2,1)}, u32[]{:S(2)}, u32[]{:S(2)}) collective-permute-start(bf16[128,1024]{0,1:T(8,128)(2,1)S(1)} %bitcast.284), channel_id=1, source_target_pairs={{0,6},{1,7},{2,0},{3,1},{4,2},{5,3},{6,4},{7,5},{8,14},{9,15},{10,... | collective-permute-start | bytes 786440 | tf_op jit(solution)/shard_map/ppermute | solution.py:328
  66.7 34.2 %collective-permute-start.25 = (bf16[128,1024]{0,1:T(8,128)(2,1)S(1)}, bf16[128,1024]{0,1:T(8,128)(2,1)}, u32[]{:S(2)}, u32[]{:S(2)}) collective-permute-start(bf16[128,1024]{0,1:T(8,128)(2,1)S(1)} %bitcast.285), channel_id=1, source_target_pairs={{0,4},{1,5},{2,6},{3,7},{4,0},{5,1},{6,2},{7,3},{8,12},{9,13},{10,... | collective-permute-start | bytes 786440 | tf_op jit(solution)/shard_map/ppermute | solution.py:328
  68.4 18.1 %copy-start.39 = (bf16[1,128,384]{2,1,0:T(8,128)(2,1)S(1)}, bf16[1,128,384]{2,1,0:T(8,128)(2,1)}, u32[]{:S(2)}) copy-start(bf16[1,128,384]{2,1,0:T(8,128)(2,1)} %copy.66) | copy-start | bytes 294916
  68.4 21.5 %collective-permute-start.24 = (bf16[128,1024]{0,1:T(8,128)(2,1)S(1)}, bf16[128,1024]{0,1:T(8,128)(2,1)S(1)}, u32[]{:S(2)}, u32[]{:S(2)}) collective-permute-start(bf16[128,1024]{0,1:T(8,128)(2,1)S(1)} %bitcast.286), channel_id=1, source_target_pairs={{0,2},{1,3},{2,4},{3,5},{4,6},{5,7},{6,0},{7,1},{8,10},{9,11},{10,... | collective-permute-start | bytes 786440 | tf_op jit(solution)/shard_map/ppermute | solution.py:328
  72.0 34.5 %collective-permute-start.29 = (bf16[128,1024]{1,0:T(8,128)(2,1)}, bf16[128,1024]{1,0:T(8,128)(2,1)}, u32[]{:S(2)}, u32[]{:S(2)}) collective-permute-start(bf16[128,1024]{1,0:T(8,128)(2,1)} %get-tuple-element.57), channel_id=1, source_target_pairs={{0,4},{1,5},{2,6},{3,7},{4,0},{5,1},{6,2},{7,3},{8,12},{9,13},{10,... | collective-permute-start | bytes 786440 | tf_op jit(solution)/shard_map/ppermute | solution.py:328
  77.6 16.6 %collective-permute-start.28 = (bf16[128,1024]{1,0:T(8,128)(2,1)}, bf16[128,1024]{1,0:T(8,128)(2,1)}, u32[]{:S(2)}, u32[]{:S(2)}) collective-permute-start(bf16[128,1024]{1,0:T(8,128)(2,1)} %get-tuple-element.57), channel_id=1, source_target_pairs={{0,2},{1,3},{2,4},{3,5},{4,6},{5,7},{6,0},{7,1},{8,10},{9,11},{10,... | collective-permute-start | bytes 786440 | tf_op jit(solution)/shard_map/ppermute | solution.py:328
  90.6 19.7 %collective-permute-start.30 = (bf16[128,1024]{1,0:T(8,128)(2,1)}, bf16[128,1024]{1,0:T(8,128)(2,1)}, u32[]{:S(2)}, u32[]{:S(2)}) collective-permute-start(bf16[128,1024]{1,0:T(8,128)(2,1)} %get-tuple-element.57), channel_id=1, source_target_pairs={{0,6},{1,7},{2,0},{3,1},{4,2},{5,3},{6,4},{7,5},{8,14},{9,15},{10,... | collective-permute-start | bytes 786440 | tf_op jit(solution)/shard_map/ppermute | solution.py:328
  94.2 42.6 %collective-permute-start = (bf16[512,1024]{1,0:T(8,128)(2,1)}, bf16[512,1024]{1,0:T(8,128)(2,1)}, u32[]{:S(2)}, u32[]{:S(2)}) collective-permute-start(bf16[512,1024]{1,0:T(8,128)(2,1)} %get-tuple-element.55), channel_id=1, source_target_pairs={{0,8},{8,0},{16,24},{24,16},{1,9},{9,1},{17,25},{25,17},{2,10},{10... | collective-permute-start | bytes 3145736 | tf_op jit(solution)/shard_map/ppermute | solution.py:313
  97.5 38.7 %collective-permute-start.1 = (bf16[512,1024]{1,0:T(8,128)(2,1)}, bf16[512,1024]{1,0:T(8,128)(2,1)}, u32[]{:S(2)}, u32[]{:S(2)}) collective-permute-start(bf16[512,1024]{1,0:T(8,128)(2,1)} %get-tuple-element.55), channel_id=1, source_target_pairs={{0,16},{8,24},{16,0},{24,8},{1,17},{9,25},{17,1},{25,9},{2,18},{10... | collective-permute-start | bytes 3145736 | tf_op jit(solution)/shard_map/ppermute | solution.py:313
  101.0 19.3 %collective-permute-start.20 = (bf16[4,32,1024]{2,1,0:T(8,128)(2,1)}, bf16[4,32,1024]{2,1,0:T(8,128)(2,1)}, u32[]{:S(2)}, u32[]{:S(2)}) collective-permute-start(bf16[4,32,1024]{2,1,0:T(8,128)(2,1)} %bitcast_dynamic-update-slice_fusion.20), channel_id=1, source_target_pairs={{0,1},{1,0},{2,3},{3,2},{4,5},{5,4},{6,7},{7,6},{8,9},{9,8},{10,11... | collective-permute-start | bytes 786440 | tf_op jit(solution)/shard_map/ppermute | solution.py:313
  106.5 16.9 %collective-permute-start.6 = (bf16[4,128,384]{2,1,0:T(8,128)(2,1)}, bf16[4,128,384]{2,1,0:T(8,128)(2,1)S(1)}, u32[]{:S(2)}, u32[]{:S(2)}) collective-permute-start(bf16[4,128,384]{2,1,0:T(8,128)(2,1)} %constant_dynamic-update-slice_fusion.18), channel_id=1, source_target_pairs={{0,1},{1,0},{2,3},{3,2},{4,5},{5,4},{6,7},{7,6},{8,9},{9,8},{10,11... | collective-permute-start | bytes 1179656 | tf_op jit(solution)/shard_map/ppermute | solution.py:313
  110.3 16.0 %collective-permute-start.13 = (bf16[4,128,384]{2,1,0:T(8,128)(2,1)}, bf16[4,128,384]{2,1,0:T(8,128)(2,1)S(1)}, u32[]{:S(2)}, u32[]{:S(2)}) collective-permute-start(bf16[4,128,384]{2,1,0:T(8,128)(2,1)} %bitcast_dynamic-update-slice_fusion.17), channel_id=1, source_target_pairs={{0,1},{1,0},{2,3},{3,2},{4,5},{5,4},{6,7},{7,6},{8,9},{9,8},{10,11... | collective-permute-start | bytes 1179656 | tf_op jit(solution)/shard_map/ppermute | solution.py:313
  121.9 13.8 %collective-permute-start.22 = (bf16[8,32,1024]{2,1,0:T(8,128)(2,1)}, bf16[8,32,1024]{2,1,0:T(8,128)(2,1)S(1)}, u32[]{:S(2)}, u32[]{:S(2)}) collective-permute-start(bf16[8,32,1024]{2,1,0:T(8,128)(2,1)} %bitcast.38), channel_id=1, source_target_pairs={{0,16},{8,24},{16,0},{24,8},{1,17},{9,25},{17,1},{25,9},{2,18},{10... | collective-permute-start | bytes 1572872 | tf_op jit(solution)/shard_map/ppermute | solution.py:313
  123.4 12.7 %collective-permute-start.21 = (bf16[8,32,1024]{2,1,0:T(8,128)(2,1)}, bf16[8,32,1024]{2,1,0:T(8,128)(2,1)S(1)}, u32[]{:S(2)}, u32[]{:S(2)}) collective-permute-start(bf16[8,32,1024]{2,1,0:T(8,128)(2,1)} %bitcast.38), channel_id=1, source_target_pairs={{0,8},{8,0},{16,24},{24,16},{1,9},{9,1},{17,25},{25,17},{2,10},{10... | collective-permute-start | bytes 1572872 | tf_op jit(solution)/shard_map/ppermute | solution.py:313
  126.3 26.1 %collective-permute-start.27 = (bf16[4,128,1024]{2,1,0:T(8,128)(2,1)S(1)}, bf16[4,128,1024]{2,1,0:T(8,128)(2,1)S(1)}, u32[]{:S(2)}, u32[]{:S(2)}) collective-permute-start(bf16[4,128,1024]{2,1,0:T(8,128)(2,1)S(1)} %copy-done.24), channel_id=1, source_target_pairs={{0,1},{1,0},{2,3},{3,2},{4,5},{5,4},{6,7},{7,6},{8,9},{9,8},{10,11... | collective-permute-start | bytes 3145736 | tf_op jit(solution)/shard_map/ppermute | solution.py:313
  135.7 37.4 %collective-permute-start.31 = (bf16[4,128,1024]{2,1,0:T(8,128)(2,1)}, bf16[4,128,1024]{2,1,0:T(8,128)(2,1)S(1)}, u32[]{:S(2)}, u32[]{:S(2)}) collective-permute-start(bf16[4,128,1024]{2,1,0:T(8,128)(2,1)} %bitcast_dynamic-update-slice_fusion.12), channel_id=1, source_target_pairs={{0,1},{1,0},{2,3},{3,2},{4,5},{5,4},{6,7},{7,6},{8,9},{9,8},{10,11... | collective-permute-start | bytes 3145736 | tf_op jit(solution)/shard_map/ppermute | solution.py:313
  136.1 70.1 %collective-permute-start.23 = (bf16[8,32,1024]{2,1,0:T(8,128)(2,1)S(1)}, bf16[8,32,1024]{2,1,0:T(8,128)(2,1)}, u32[]{:S(2)}, u32[]{:S(2)}) collective-permute-start(bf16[8,32,1024]{2,1,0:T(8,128)(2,1)S(1)} %collective-permute-done.22), channel_id=1, source_target_pairs={{0,8},{8,0},{16,24},{24,16},{1,9},{9,1},{17,25},{25,17},{2,10},{10... | collective-permute-start | bytes 1572872 | tf_op jit(solution)/shard_map/ppermute | solution.py:313
  136.2 37.9 %collective-permute-start.2 = (bf16[512,1024]{1,0:T(8,128)(2,1)}, bf16[512,1024]{1,0:T(8,128)(2,1)S(1)}, u32[]{:S(2)}, u32[]{:S(2)}) collective-permute-start(bf16[512,1024]{1,0:T(8,128)(2,1)} %collective-permute-done.1), channel_id=1, source_target_pairs={{0,8},{8,0},{16,24},{24,16},{1,9},{9,1},{17,25},{25,17},{2,10},{10... | collective-permute-start | bytes 3145736 | tf_op jit(solution)/shard_map/ppermute | solution.py:313
  153.5 121.2 %collective-permute-start.34 = (bf16[8,128,1024]{2,1,0:T(8,128)(2,1)}, bf16[8,128,1024]{2,1,0:T(8,128)(2,1)}, u32[]{:S(2)}, u32[]{:S(2)}) collective-permute-start(bf16[8,128,1024]{2,1,0:T(8,128)(2,1)} %bitcast.65), channel_id=1, source_target_pairs={{0,16},{8,24},{16,0},{24,8},{1,17},{9,25},{17,1},{25,9},{2,18},{10... | collective-permute-start | bytes 6291464 | tf_op jit(solution)/shard_map/ppermute | solution.py:313
  154.0 124.5 %collective-permute-start.32 = (bf16[8,128,1024]{2,1,0:T(8,128)(2,1)}, bf16[8,128,1024]{2,1,0:T(8,128)(2,1)}, u32[]{:S(2)}, u32[]{:S(2)}) collective-permute-start(bf16[8,128,1024]{2,1,0:T(8,128)(2,1)} %bitcast.65), channel_id=1, source_target_pairs={{0,8},{8,0},{16,24},{24,16},{1,9},{9,1},{17,25},{25,17},{2,10},{10... | collective-permute-start | bytes 6291464 | tf_op jit(solution)/shard_map/ppermute | solution.py:313
  190.9 10.2 %collective-permute-start.8 = (bf16[512,128]{1,0:T(8,128)(2,1)S(1)}, bf16[512,128]{1,0:T(8,128)(2,1)S(1)}, u32[]{:S(2)}, u32[]{:S(2)}) collective-permute-start(bf16[512,128]{1,0:T(8,128)(2,1)S(1)} %get-tuple-element.72), channel_id=1, source_target_pairs={{0,16},{8,24},{16,0},{24,8},{1,17},{9,25},{17,1},{25,9},{2,18},{10... | collective-permute-start | bytes 393224 | tf_op jit(solution)/shard_map/ppermute | solution.py:313
  191.4 7.9 %collective-permute-start.7 = (bf16[512,128]{1,0:T(8,128)(2,1)S(1)}, bf16[512,128]{1,0:T(8,128)(2,1)S(1)}, u32[]{:S(2)}, u32[]{:S(2)}) collective-permute-start(bf16[512,128]{1,0:T(8,128)(2,1)S(1)} %get-tuple-element.73), channel_id=1, source_target_pairs={{0,8},{8,0},{16,24},{24,16},{1,9},{9,1},{17,25},{25,17},{2,10},{10... | collective-permute-start | bytes 393224 | tf_op jit(solution)/shard_map/ppermute | solution.py:313
  199.3 57.2 %copy-start.3 = (bf16[2048,128]{1,0:T(8,128)(2,1)}, bf16[2048,128]{1,0:T(8,128)(2,1)S(1)}, u32[]{:S(2)}) copy-start(bf16[2048,128]{1,0:T(8,128)(2,1)S(1)} %get-tuple-element.17.o_ref) | copy-start | bytes 1572868
  199.3 57.2 %copy-start.11 = (bf16[2048,128]{1,0:T(8,128)(2,1)}, bf16[2048,128]{1,0:T(8,128)(2,1)S(1)}, u32[]{:S(2)}) copy-start(bf16[2048,128]{1,0:T(8,128)(2,1)S(1)} %get-tuple-element.20.stat_ref) | copy-start | bytes 1572868
  199.3 55.9 %copy-start.18 = (bf16[1,512,1024]{2,1,0:T(8,128)(2,1)S(1)}, bf16[1,512,1024]{2,1,0:T(8,128)(2,1)}, u32[]{:S(2)}) copy-start(bf16[1,512,1024]{2,1,0:T(8,128)(2,1)} %param.12) | copy-start | bytes 3145732
  199.3 5.5 %collective-permute-start.9 = (bf16[512,128]{1,0:T(8,128)(2,1)S(1)}, bf16[512,128]{1,0:T(8,128)(2,1)S(1)}, u32[]{:S(2)}, u32[]{:S(2)}) collective-permute-start(bf16[512,128]{1,0:T(8,128)(2,1)S(1)} %get-tuple-element.71), channel_id=1, source_target_pairs={{0,24},{8,16},{16,8},{24,0},{1,25},{9,17},{17,9},{25,1},{2,26},{10... | collective-permute-start | bytes 393224 | tf_op jit(solution)/shard_map/ppermute | solution.py:313
  201.0 74.1 %collective-permute-start.35 = (bf16[8,128,1024]{2,1,0:T(8,128)(2,1)}, bf16[8,128,1024]{2,1,0:T(8,128)(2,1)}, u32[]{:S(2)}, u32[]{:S(2)}) collective-permute-start(bf16[8,128,1024]{2,1,0:T(8,128)(2,1)} %bitcast.67), channel_id=1, source_target_pairs={{0,16},{8,24},{16,0},{24,8},{1,17},{9,25},{17,1},{25,9},{2,18},{10... | collective-permute-start | bytes 6291464 | tf_op jit(solution)/shard_map/ppermute | solution.py:313
  205.0 48.6 %collective-permute-start.15 = (bf16[512,128]{1,0:T(8,128)(2,1)S(1)}, bf16[512,128]{1,0:T(8,128)(2,1)S(1)}, u32[]{:S(2)}, u32[]{:S(2)}) collective-permute-start(bf16[512,128]{1,0:T(8,128)(2,1)S(1)} %get-tuple-element.68), channel_id=1, source_target_pairs={{0,16},{8,24},{16,0},{24,8},{1,17},{9,25},{17,1},{25,9},{2,18},{10... | collective-permute-start | bytes 393224 | tf_op jit(solution)/shard_map/ppermute | solution.py:313
  206.3 1.9 collective-permute-start.14
  208.1 48.4 %copy-start.27 = (bf16[8,4,32,1024]{3,2,1,0:T(8,128)(2,1)}, bf16[8,4,32,1024]{3,2,1,0:T(8,128)(2,1)S(1)}, u32[]{:S(2)}) copy-start(bf16[8,4,32,1024]{3,2,1,0:T(8,128)(2,1)S(1)} %bitcast_dynamic-update-slice_fusion.4) | copy-start | bytes 6291460
  208.2 47.0 %collective-permute-start.16 = (bf16[512,128]{1,0:T(8,128)(2,1)S(1)}, bf16[512,128]{1,0:T(8,128)(2,1)S(1)}, u32[]{:S(2)}, u32[]{:S(2)}) collective-permute-start(bf16[512,128]{1,0:T(8,128)(2,1)S(1)} %get-tuple-element.67), channel_id=1, source_target_pairs={{0,24},{8,16},{16,8},{24,0},{1,25},{9,17},{17,9},{25,1},{2,26},{10... | collective-permute-start | bytes 393224 | tf_op jit(solution)/shard_map/ppermute | solution.py:313
  253.5 33.7 %collective-permute-start.33 = (bf16[8,128,1024]{2,1,0:T(8,128)(2,1)}, bf16[8,128,1024]{2,1,0:T(8,128)(2,1)}, u32[]{:S(2)}, u32[]{:S(2)}) collective-permute-start(bf16[8,128,1024]{2,1,0:T(8,128)(2,1)} %bitcast.67), channel_id=1, source_target_pairs={{0,8},{8,0},{16,24},{24,16},{1,9},{9,1},{17,25},{25,17},{2,10},{10... | collective-permute-start | bytes 6291464 | tf_op jit(solution)/shard_map/ppermute | solution.py:313
  274.7 32.7 %collective-permute-start.36 = (bf16[8,128,1024]{2,1,0:T(8,128)(2,1)}, bf16[8,128,1024]{2,1,0:T(8,128)(2,1)}, u32[]{:S(2)}, u32[]{:S(2)}) collective-permute-start(bf16[8,128,1024]{2,1,0:T(8,128)(2,1)} %collective-permute-done.34), channel_id=1, source_target_pairs={{0,8},{8,0},{16,24},{24,16},{1,9},{9,1},{17,25},{25,17},{2,10},{10... | collective-permute-start | bytes 6291464 | tf_op jit(solution)/shard_map/ppermute | solution.py:313
  275.2 36.7 %collective-permute-start.37 = (bf16[8,128,1024]{2,1,0:T(8,128)(2,1)}, bf16[8,128,1024]{2,1,0:T(8,128)(2,1)}, u32[]{:S(2)}, u32[]{:S(2)}) collective-permute-start(bf16[8,128,1024]{2,1,0:T(8,128)(2,1)} %collective-permute-done.35), channel_id=1, source_target_pairs={{0,8},{8,0},{16,24},{24,16},{1,9},{9,1},{17,25},{25,17},{2,10},{10... | collective-permute-start | bytes 6291464 | tf_op jit(solution)/shard_map/ppermute | solution.py:313
  327.2 14.3 %collective-permute-start.40 = (bf16[512,128]{1,0:T(8,128)(2,1)S(1)}, bf16[512,128]{1,0:T(8,128)(2,1)S(1)}, u32[]{:S(2)}, u32[]{:S(2)}) collective-permute-start(bf16[512,128]{1,0:T(8,128)(2,1)S(1)} %get-tuple-element.60), channel_id=1, source_target_pairs={{0,24},{8,16},{16,8},{24,0},{1,25},{9,17},{17,9},{25,1},{2,26},{10... | collective-permute-start | bytes 393224 | tf_op jit(solution)/shard_map/ppermute | solution.py:313
  328.9 12.7 %collective-permute-start.43 = (bf16[512,128]{1,0:T(8,128)(2,1)S(1)}, bf16[512,128]{1,0:T(8,128)(2,1)S(1)}, u32[]{:S(2)}, u32[]{:S(2)}) collective-permute-start(bf16[512,128]{1,0:T(8,128)(2,1)S(1)} %get-tuple-element.61), channel_id=1, source_target_pairs={{0,24},{8,16},{16,8},{24,0},{1,25},{9,17},{17,9},{25,1},{2,26},{10... | collective-permute-start | bytes 393224 | tf_op jit(solution)/shard_map/ppermute | solution.py:313
  329.0 10.2 %collective-permute-start.42 = (bf16[512,128]{1,0:T(8,128)(2,1)S(1)}, bf16[512,128]{1,0:T(8,128)(2,1)S(1)}, u32[]{:S(2)}, u32[]{:S(2)}) collective-permute-start(bf16[512,128]{1,0:T(8,128)(2,1)S(1)} %get-tuple-element.62), channel_id=1, source_target_pairs={{0,16},{8,24},{16,0},{24,8},{1,17},{9,25},{17,1},{25,9},{2,18},{10... | collective-permute-start | bytes 393224 | tf_op jit(solution)/shard_map/ppermute | solution.py:313
  330.6 5.0 %collective-permute-start.41 = (bf16[512,128]{1,0:T(8,128)(2,1)S(1)}, bf16[512,128]{1,0:T(8,128)(2,1)S(1)}, u32[]{:S(2)}, u32[]{:S(2)}) collective-permute-start(bf16[512,128]{1,0:T(8,128)(2,1)S(1)} %get-tuple-element.63), channel_id=1, source_target_pairs={{0,8},{8,0},{16,24},{24,16},{1,9},{9,1},{17,25},{25,17},{2,10},{10... | collective-permute-start | bytes 393224 | tf_op jit(solution)/shard_map/ppermute | solution.py:313
  330.7 10.8 %collective-permute-start.39 = (bf16[512,128]{1,0:T(8,128)(2,1)S(1)}, bf16[512,128]{1,0:T(8,128)(2,1)S(1)}, u32[]{:S(2)}, u32[]{:S(2)}) collective-permute-start(bf16[512,128]{1,0:T(8,128)(2,1)S(1)} %get-tuple-element.65), channel_id=1, source_target_pairs={{0,16},{8,24},{16,0},{24,8},{1,17},{9,25},{17,1},{25,9},{2,18},{10... | collective-permute-start | bytes 393224 | tf_op jit(solution)/shard_map/ppermute | solution.py:313
  335.6 3.7 collective-permute-start.38
  341.6 15.5 %copy-start.4 = (bf16[2048,128]{1,0:T(8,128)(2,1)S(1)}, bf16[2048,128]{1,0:T(8,128)(2,1)}, u32[]{:S(2)}) copy-start(bf16[2048,128]{1,0:T(8,128)(2,1)} %copy-done.3) | copy-start | bytes 1572868
  341.7 15.5 %copy-start.6 = (bf16[2048,384]{1,0:T(8,128)(2,1)S(1)}, bf16[2048,384]{1,0:T(8,128)(2,1)}, u32[]{:S(2)}) copy-start(bf16[2048,384]{1,0:T(8,128)(2,1)} %copy-done.5) | copy-start | bytes 4718596
  341.7 15.5 %copy-start.12 = (bf16[2048,128]{1,0:T(8,128)(2,1)S(1)}, bf16[2048,128]{1,0:T(8,128)(2,1)}, u32[]{:S(2)}) copy-start(bf16[2048,128]{1,0:T(8,128)(2,1)} %copy-done.11) | copy-start | bytes 1572868
  372.3 22.0 %collective-permute-start.47 = (f32[2,16,2,128]{3,1,0,2:T(8,128)S(1)}, f32[2,16,2,128]{3,1,0,2:T(8,128)S(1)}, u32[]{:S(2)}, u32[]{:S(2)}) collective-permute-start(f32[2,16,2,128]{3,1,0,2:T(8,128)S(1)} %pad_maximum_fusion), channel_id=1, source_target_pairs={{0,4},{1,5},{2,6},{3,7},{4,0},{5,1},{6,2},{7,3},{8,12},{9,13},{10,... | collective-permute-start | bytes 98312 | tf_op jit(solution)/shard_map/ppermute | solution.py:313
  394.3 4.0 collective-permute-start.48
  398.3 5.1 %collective-permute-start.49 = (f32[2,16,2,128]{3,1,0,2:T(8,128)S(1)}, f32[2,16,2,128]{3,1,0,2:T(8,128)S(1)}, u32[]{:S(2)}, u32[]{:S(2)}) collective-permute-start(f32[2,16,2,128]{3,1,0,2:T(8,128)S(1)} %fusion.197), channel_id=1, source_target_pairs={{0,1},{1,0},{2,3},{3,2},{4,5},{5,4},{6,7},{7,6},{8,9},{9,8},{10,11... | collective-permute-start | bytes 98312 | tf_op jit(solution)/shard_map/ppermute | solution.py:313
  402.9 30.8 %collective-permute-start.44 = (bf16[512,1024]{1,0:T(8,128)(2,1)}, bf16[512,1024]{1,0:T(8,128)(2,1)S(1)}, u32[]{:S(2)}, u32[]{:S(2)}) collective-permute-start(bf16[512,1024]{1,0:T(8,128)(2,1)} %get-tuple-element.58), channel_id=1, source_target_pairs={{0,8},{8,0},{16,24},{24,16},{1,9},{9,1},{17,25},{25,17},{2,10},{10... | collective-permute-start | bytes 3145736 | tf_op jit(solution)/shard_map/ppermute | solution.py:313
  402.9 7.3 %collective-permute-start.45 = (bf16[512,1024]{1,0:T(8,128)(2,1)}, bf16[512,1024]{1,0:T(8,128)(2,1)}, u32[]{:S(2)}, u32[]{:S(2)}) collective-permute-start(bf16[512,1024]{1,0:T(8,128)(2,1)} %get-tuple-element.59), channel_id=1, source_target_pairs={{0,8},{8,0},{16,24},{24,16},{1,9},{9,1},{17,25},{25,17},{2,10},{10... | collective-permute-start | bytes 3145736 | tf_op jit(solution)/shard_map/ppermute | solution.py:313
  403.4 4.0 collective-permute-start.51
  405.0 2.4 collective-permute-start.50
  407.4 1.2 collective-permute-start.52
  413.6 25.5 %collective-permute-start.46 = (bf16[512,1024]{1,0:T(8,128)(2,1)}, bf16[512,1024]{1,0:T(8,128)(2,1)}, u32[]{:S(2)}, u32[]{:S(2)}) collective-permute-start(bf16[512,1024]{1,0:T(8,128)(2,1)} %add_convert_fusion.1), channel_id=1, source_target_pairs={{0,16},{8,24},{16,0},{24,8},{1,17},{9,25},{17,1},{25,9},{2,18},{10... | collective-permute-start | bytes 3145736 | tf_op jit(solution)/shard_map/ppermute | solution.py:313
  (37 other events, 181.1 us)

commit v2 on v1

v2 whole, which is shorter than its diff:
```python
import functools

import jax
import jax.numpy as jnp
from jax import lax
from jax.experimental import pallas as pl
from jax.experimental.pallas import tpu as pltpu
from jax.sharding import PartitionSpec as P

PREFIX = 10
HEAD = 64
PAIR = 128
PREFIX_ROWS = 16
VT_ROWS = 80
blocked = -1e30
norm_epsilon = 1e-05
highest = lax.Precision.HIGHEST
f32, bf16 = jnp.float32, jnp.bfloat16
VMEM_LIMIT = 56 << 20
in_vmem = pl.BlockSpec(memory_space=pltpu.VMEM)
in_smem = pl.BlockSpec(memory_space=pltpu.SMEM)
in_place = pl.BlockSpec(memory_space=pl.ANY)


def params():
    return pltpu.CompilerParams(vmem_limit_bytes=VMEM_LIMIT)


def cost(flops, moved, special=0):
    return pl.CostEstimate(flops=int(flops), bytes_accessed=int(moved), transcendentals=int(special))


def like(shape, dtype=bf16):
    return jax.ShapeDtypeStruct(shape, dtype)


def dot(a, b, ca, cb):
    return lax.dot_general(a, b, (((ca,), (cb,)), ((), ())), preferred_element_type=f32)


def lane(shape):
    return lax.broadcasted_iota(jnp.int32, shape, len(shape) - 1)


def head_half(h, shape):
    l = lane(shape)
    return (l < HEAD) if h == 0 else (l >= HEAD)


def split3(v):
    hi = v.astype(bf16)
    r = v - hi.astype(f32)
    mid = r.astype(bf16)
    lo = (r - mid.astype(f32)).astype(bf16)
    return hi.astype(f32), mid.astype(f32), lo.astype(f32)


def at(index, size):
    return pl.ds(pl.multiple_of(index * size, size), size)


def normalize(hidden):
    centered = hidden - jnp.mean(hidden, axis=-1, keepdims=True)
    scale = lax.rsqrt(jnp.mean(centered * centered, axis=-1, keepdims=True) + norm_epsilon)
    return centered * scale, scale


def normalize_back(normed, scale, grad):
    return scale * (
        grad
        - jnp.mean(grad, axis=-1, keepdims=True)
        - normed * jnp.mean(grad * normed, axis=-1, keepdims=True)
    )


def cut_attend_body(seq, pairs, place, attend_ref, *outs):
    width = attend_ref.shape[1] // 3
    for p in range(pairs):
        for t in range(3):
            column = t * width + (place[0] * pairs + p) * PAIR
            outs[p][:, t * PAIR : (t + 1) * PAIR] = attend_ref[
                :, pl.ds(pl.multiple_of(column, PAIR), PAIR)
            ]


def cut_attend(seq, pairs, place, attend_weight):
    rows = attend_weight.shape[0]
    return pl.pallas_call(
        functools.partial(cut_attend_body, seq, pairs),
        in_specs=[in_smem, in_vmem],
        out_specs=[in_vmem] * pairs,
        out_shape=[like((rows, 3 * PAIR))] * pairs,
        cost_estimate=cost(0, attend_weight.size * 3),
        compiler_params=params(),
        name="cut_attend",
    )(place, attend_weight)


def cut_rest_body(seq, place, output_ref, expand_ref, shrink_ref, up_ref, down_ref):
    s = place[0]
    wide = output_ref.shape[1] // seq
    up_ref[:, :wide] = output_ref[:, at(s, wide)]
    up_ref[:, wide:] = expand_ref[:, at(s, expand_ref.shape[1] // seq)]
    part = shrink_ref.shape[0] // seq
    for x in range(seq // 2):
        down_ref[x * part : (x + 1) * part, :] = shrink_ref[at(2 * x + lax.rem(s, 2), part), :]


def cut_rest(seq, place, output_weight, expand_weight, shrink_weight):
    rows, width = output_weight.shape
    up_shape = (rows, (width + expand_weight.shape[1]) // seq)
    return pl.pallas_call(
        functools.partial(cut_rest_body, seq),
        in_specs=[in_smem, in_vmem, in_vmem, in_vmem],
        out_specs=[in_vmem] * 2,
        out_shape=[like(up_shape), like((shrink_weight.shape[0] // 2, width))],
        cost_estimate=cost(0, expand_weight.size * 6),
        compiler_params=params(),
        name="cut_rest",
    )(place, output_weight, expand_weight, shrink_weight)


def forward_body(seq, bq, bk, place, *refs):
    normed, (line, other, pk_ref, pv_ref, mq_ref, mk_ref, pm_ref) = refs[:seq], refs[seq : seq + 7]
    qkv_ref, stat_ref, weight_ref = refs[seq + 7 : seq + 10]
    outs, (ka, vt, pka, pvt, qh, o_all) = refs[seq + 10 : 2 * seq + 10], refs[2 * seq + 10 :]
    s = place[0]
    s_len = qkv_ref.shape[0]
    rows = s_len // seq
    count = line.shape[0]
    shard = line.shape[1]
    for j in range(count):
        weight_ref[at(place[1 + j], shard), :] = line[j]
        weight_ref[at(place[1 + count + j], shard), :] = other[j]
    for r in range(seq):
        got = jnp.dot(normed[r][...], weight_ref[...], preferred_element_type=f32)
        qkv_ref[at(lax.bitwise_xor(s, r), rows), :] = got.astype(bf16)
    ka[:, :PAIR] = qkv_ref[:, PAIR : 2 * PAIR]
    ka[:, PAIR:] = mk_ref[...]
    pka[:, :PAIR] = pk_ref[...]
    pka[:, PAIR:] = pm_ref[...]
    first_row = lax.broadcasted_iota(jnp.int32, (VT_ROWS - HEAD, s_len), 0) == 0
    ones = jnp.where(first_row, 1.0, 0.0).astype(bf16)
    vtr = qkv_ref[:, 2 * PAIR :].T
    pvr = pv_ref[...].T
    for h in (0, 1):
        vt[h, :HEAD, :] = vtr[h * HEAD : (h + 1) * HEAD, :]
        vt[h, HEAD:, :] = ones
        pvt[h, :HEAD, :] = pvr[h * HEAD : (h + 1) * HEAD, :]
        pvt[h, HEAD:, :] = ones[:, :PREFIX_ROWS]

    def block(start, state, first, causal):
        out = []
        start = pl.multiple_of(start, bk)
        scores = [dot(ka[pl.ds(start, bk), :], qh[h, first:, :], 1, 1) for h in (0, 1)]
        for h in (0, 1):
            m, acc = state[2 * h], state[2 * h + 1]
            x = scores[h]
            if causal:
                ok = lax.broadcasted_iota(jnp.int32, x.shape, 0) <= lane(x.shape)
                x = jnp.where(ok, x, blocked)
            if first:
                keep_m, keep_acc = m[:, :first], acc[:, :first]
                m, acc = m[:, first:], acc[:, first:]
            new = jnp.maximum(m, jnp.max(x, axis=0, keepdims=True))
            p = jnp.exp(x - new)
            acc = acc * jnp.exp(m - new) + dot(vt[h, :, pl.ds(start, bk)], p.astype(bf16), 1, 0)
            if first:
                new = jnp.concatenate([keep_m, new], axis=1)
                acc = jnp.concatenate([keep_acc, acc], axis=1)
            out += [new, acc]
        return tuple(out)

    for i in range(s_len // bq):
        span = slice(i * bq, (i + 1) * bq)
        q = qkv_ref[span, :PAIR] * bf16(0.125)
        for h in (0, 1):
            qh[h, :, :PAIR] = jnp.where(head_half(h, q.shape), q, bf16(0))
            qh[h, :, PAIR:] = mq_ref[span, :]
        state = []
        for h in (0, 1):
            x = dot(pka[...], qh[h], 1, 1)
            m = jnp.max(x, axis=0, keepdims=True)
            state += [m, dot(pvt[h], jnp.exp(x - m).astype(bf16), 1, 0)]
        state = tuple(state)
        if i:
            state = lax.fori_loop(
                0, i * (bq // bk), lambda j, st: block(j * bk, st, 0, False), state
            )
        for j in range(bq // bk):
            state = block(i * bq + j * bk, state, j * bk, True)
        tops, parts = [], []
        for h in (0, 1):
            m, acc = state[2 * h], state[2 * h + 1]
            total = acc[HEAD : HEAD + 1]
            tops.append(acc[:HEAD] / total)
            parts += split3(-(m + jnp.log(total)))
        o_all[span, :] = jnp.concatenate(tops, axis=0).T.astype(bf16)
        pad = jnp.zeros((PAIR - 4 - len(parts), bq), f32)
        logs = jnp.concatenate([jnp.zeros((4, bq), f32)] + parts + [pad], axis=0).T
        stat_ref[span, :] = (logs + mq_ref[span, :].astype(f32)).astype(bf16)
    for r in range(seq):
        outs[r][...] = o_all[at(lax.bitwise_xor(s, r), rows), :]


def attend_forward(place, normed, line, other, pk, pv, mq, mk, pm):
    seq = len(normed)
    rows, width = normed[0].shape
    s_len = rows * seq
    bq, bk = min(2048, s_len), min(512, s_len)
    return pl.pallas_call(
        functools.partial(forward_body, seq, bq, bk),
        in_specs=[in_smem] + [in_vmem] * (seq + 7),
        out_specs=[in_vmem] * (3 + seq),
        out_shape=[like((s_len, 3 * PAIR)), like((s_len, PAIR)), like((width, 3 * PAIR))]
        + [like((rows, PAIR))] * seq,
        scratch_shapes=[
            pltpu.VMEM((s_len, 2 * PAIR), bf16),
            pltpu.VMEM((2, VT_ROWS, s_len), bf16),
            pltpu.VMEM((PREFIX_ROWS, 2 * PAIR), bf16),
            pltpu.VMEM((2, VT_ROWS, PREFIX_ROWS), bf16),
            pltpu.VMEM((2, bq, 2 * PAIR), bf16),
            pltpu.VMEM((s_len, PAIR), bf16),
        ],
        compiler_params=params(),
        cost_estimate=cost(
            2 * s_len * s_len * 512 + 2 * s_len * width * 3 * PAIR, s_len * width * 3, s_len * s_len
        ),
        name="attend_forward",
    )(place, *normed, line, other, pk, pv, mq, mk, pm)


def backward_body(seq, bq, bk, place, *refs):
    (qkv_ref, pk_ref, pv_ref, stat_ref, mk_ref, pm_ref), refs = refs[:6], refs[6:]
    o_parts, do_parts, refs = refs[:seq], refs[seq : 2 * seq], refs[2 * seq :]
    grad_refs, (dp_ref,), refs = refs[:seq], refs[seq : seq + 1], refs[seq + 1 :]
    ka, va, kt, pka, pva, pkt, qh, dh, dk_acc, dv_acc, o_all, do_all, dq_all = refs
    s = place[0]
    s_len = qkv_ref.shape[0]
    rows = s_len // seq
    for r in range(seq):
        o_all[at(lax.bitwise_xor(s, r), rows), :] = o_parts[r][...]
        do_all[at(lax.bitwise_xor(s, r), rows), :] = do_parts[r][...]
    ones = jnp.where(lane((s_len, PAIR)) < 3, 1.0, 0.0).astype(bf16)
    l = lane((s_len, PAIR))
    k = qkv_ref[:, PAIR : 2 * PAIR]
    for h in (0, 1):
        mine = (l >= 4 + 3 * h) & (l < 7 + 3 * h)
        ka[h, :, :PAIR] = k
        ka[h, :, PAIR:] = jnp.where(mine, bf16(1), mk_ref[...])
        pka[h, :, :PAIR] = pk_ref[...]
        pka[h, :, PAIR:] = jnp.where(mine[:PREFIX_ROWS], bf16(1), pm_ref[...])
    va[:, :PAIR] = qkv_ref[:, 2 * PAIR :]
    va[:, PAIR:] = ones
    pva[:, :PAIR] = pv_ref[...]
    pva[:, PAIR:] = ones[:PREFIX_ROWS]
    kt[...] = k.T
    pkt[...] = pk_ref[...].T
    dk_acc[...] = jnp.zeros_like(dk_acc)
    dv_acc[...] = jnp.zeros_like(dv_acc)

    def block(start, state, first, causal):
        start = pl.multiple_of(start, bk)
        here = pl.ds(start, bk)
        out = []
        dv = dk = None
        scores = [dot(ka[h, here, :], qh[h, first:, :], 1, 1) for h in (0, 1)]
        dps = [dot(va[here, :], dh[h, first:, :], 1, 1) for h in (0, 1)]
        for h in (0, 1):
            p = jnp.exp(scores[h])
            if causal:
                ok = lax.broadcasted_iota(jnp.int32, p.shape, 0) <= lane(p.shape)
                p = jnp.where(ok, p, 0.0)
            ds = (p * dps[h]).astype(bf16)
            a = dot(p.astype(bf16), dh[h, first:, :PAIR], 1, 0)
            b = dot(ds, qh[h, first:, :PAIR], 1, 0)
            dv = a if dv is None else dv + a
            dk = b if dk is None else dk + b
            c = dot(kt[h * HEAD : (h + 1) * HEAD, here], ds, 1, 0)
            if first:
                out.append(jnp.concatenate([state[h][:, :first], state[h][:, first:] + c], axis=1))
            else:
                out.append(state[h] + c)
        dv_acc[here, :] += dv
        dk_acc[here, :] += dk
        return tuple(out)

    for i in range(s_len // bq):
        span = slice(i * bq, (i + 1) * bq)
        q = qkv_ref[span, :PAIR] * bf16(0.125)
        do = do_all[span, :]
        prod = do.astype(f32) * o_all[span, :].astype(f32)
        for h in (0, 1):
            half = head_half(h, q.shape)
            qh[h, :, :PAIR] = jnp.where(half, q, bf16(0))
            qh[h, :, PAIR:] = stat_ref[span, :]
            dh[h, :, :PAIR] = jnp.where(half, do, bf16(0))
            delta = -jnp.sum(jnp.where(half, prod, 0.0), axis=1, keepdims=True)
            hi, mid, lo = split3(delta)
            n = lane((bq, PAIR))
            dh[h, :, PAIR:] = jnp.where(
                n == 0, hi, jnp.where(n == 1, mid, jnp.where(n == 2, lo, 0.0))
            ).astype(bf16)
        state = []
        dpk = dpv = jnp.zeros((PREFIX_ROWS, PAIR), f32)
        for h in (0, 1):
            p = jnp.exp(dot(pka[h], qh[h], 1, 1))
            ds = (p * dot(pva[...], dh[h], 1, 1)).astype(bf16)
            dpv = dpv + dot(p.astype(bf16), dh[h, :, :PAIR], 1, 0)
            dpk = dpk + dot(ds, qh[h, :, :PAIR], 1, 0)
            state.append(dot(pkt[h * HEAD : (h + 1) * HEAD, :], ds, 1, 0))
        dp_ref[0] = dpk if i == 0 else dp_ref[0] + dpk
        dp_ref[1] = dpv if i == 0 else dp_ref[1] + dpv
        state = tuple(state)
        if i:
            state = lax.fori_loop(
                0, i * (bq // bk), lambda j, st: block(j * bk, st, 0, False), state
            )
        for j in range(bq // bk):
            state = block(i * bq + j * bk, state, j * bk, True)
        dq_all[span, :] = (jnp.concatenate(state, axis=0) * 0.125).T.astype(bf16)
    for r in range(seq):
        here = at(lax.bitwise_xor(s, r), rows)
        grad_refs[r][:, :PAIR] = dq_all[here, :]
        grad_refs[r][:, PAIR : 2 * PAIR] = dk_acc[here, :].astype(bf16)
        grad_refs[r][:, 2 * PAIR :] = dv_acc[here, :].astype(bf16)


def attend_backward(place, qkv, pk, pv, stat, mk, pm, o_parts, do_parts):
    seq = len(o_parts)
    s_len = qkv.shape[0]
    rows = s_len // seq
    bq, bk = min(2048, s_len), min(256, s_len)
    return pl.pallas_call(
        functools.partial(backward_body, seq, bq, bk),
        in_specs=[in_smem] + [in_vmem] * (6 + 2 * seq),
        out_specs=[in_vmem] * (seq + 1),
        out_shape=[like((rows, 3 * PAIR))] * seq + [like((2, PREFIX_ROWS, PAIR), f32)],
        scratch_shapes=[
            pltpu.VMEM((2, s_len, 2 * PAIR), bf16),
            pltpu.VMEM((s_len, 2 * PAIR), bf16),
            pltpu.VMEM((PAIR, s_len), bf16),
            pltpu.VMEM((2, PREFIX_ROWS, 2 * PAIR), bf16),
            pltpu.VMEM((PREFIX_ROWS, 2 * PAIR), bf16),
            pltpu.VMEM((PAIR, PREFIX_ROWS), bf16),
            pltpu.VMEM((2, bq, 2 * PAIR), bf16),
            pltpu.VMEM((2, bq, 2 * PAIR), bf16),
            pltpu.VMEM((s_len, PAIR), f32),
            pltpu.VMEM((s_len, PAIR), f32),
            pltpu.VMEM((s_len, PAIR), bf16),
            pltpu.VMEM((s_len, PAIR), bf16),
            pltpu.VMEM((s_len, PAIR), bf16),
        ],
        compiler_params=params(),
        cost_estimate=cost(5 * s_len * s_len * 512, s_len * PAIR * 24, s_len * s_len),
        name="attend_backward",
    )(place, qkv, pk, pv, stat, mk, pm, *o_parts, *do_parts)


def middle_body(seq, pairs, count, place, *refs):
    tokens_ref, cot_ref, refs = refs[0], refs[1], refs[2:]
    heads, refs = refs[: seq * pairs], refs[seq * pairs :]
    ups, refs = refs[: 2 * seq], refs[2 * seq :]
    downs, refs = refs[:4], refs[4:]
    out_ref, mid_grad_ref, refs = refs[0], refs[1], refs[2:]
    grads, refs = refs[: seq * pairs], refs[seq * pairs :]
    up, down, merged, mid, normed, out_acc, back_acc, sem_u, sem_d = refs
    s = place[0]
    rows, width = tokens_ref.shape
    shard = up.shape[1] // (2 * count)
    wide = width // seq
    part = down.shape[0] // (2 * count * seq)

    copies_u, copies_d = [], []
    for r in range(seq):
        owner = lax.bitwise_xor(s, r)
        for t in (0, 1):
            for j in range(count):
                copies_u.append(
                    pltpu.make_async_copy(
                        ups[2 * r + t].at[j],
                        up.at[owner, at(place[1 + t * count + j], shard)],
                        sem_u.at[(r * 2 + t) * count + j],
                    )
                )
    for c in (0, 1):
        owner = lax.bitwise_xor(lax.rem(s, 2), c)
        for t in (0, 1):
            for j in range(count):
                d = place[1 + t * count + j]
                for x in range(seq // 2):
                    n = ((c * 2 + t) * count + j) * (seq // 2) + x
                    first = (d * seq + 2 * x + owner) * part
                    copies_d.append(
                        pltpu.make_async_copy(
                            downs[2 * c + t].at[j, pl.ds(x * part, part)],
                            down.at[pl.ds(pl.multiple_of(first, part), part)],
                            sem_d.at[n],
                        )
                    )
    for copy in copies_u + copies_d:
        copy.start()
    for r in range(seq):
        for p in range(pairs):
            column = lax.bitwise_xor(s, r) * (pairs * PAIR) + p * PAIR
            merged[:, pl.ds(pl.multiple_of(column, PAIR), PAIR)] = heads[p * seq + r][...]
    for copy in copies_u:
        copy.wait()
    acc = tokens_ref[...].astype(f32) + jnp.concatenate(
        [dot(merged[...], up[o, :, :wide], 1, 0) for o in range(seq)], axis=1
    )
    mid[...] = acc
    normed[...] = normalize(acc)[0].astype(bf16)
    out_acc[...] = acc
    back_acc[...] = jnp.zeros_like(back_acc)
    for copy in copies_d:
        copy.wait()
    chunk = min(512, up.shape[2] - wide)
    inner = (up.shape[2] - wide) // chunk

    def step(h, carry):
        block, piece = h // inner, lax.rem(h, inner)
        w_up = up[block, :, pl.ds(pl.multiple_of(wide + piece * chunk, PAIR), chunk)]
        w_down = down[at(h, chunk), :]
        u = jnp.dot(normed[...], w_up, preferred_element_type=f32)
        gelu_grad = dot(cot_ref[...], w_down, 1, 1)
        square = u * u
        t = jnp.tanh(0.7978845608028654 * u * (1.0 + 0.044715 * square))
        half = 0.5 * (1.0 + t)
        slope = half + (0.5 * 0.7978845608028654) * u * (1.0 - t * t) * (
            1.0 + 3 * 0.044715 * square
        )
        activated = (u * half).astype(bf16)
        expand_grad = (gelu_grad * slope).astype(bf16)
        out_acc[...] += jnp.dot(activated, w_down, preferred_element_type=f32)
        back_acc[...] += dot(expand_grad, w_up, 1, 1)
        return carry

    lax.fori_loop(0, seq * inner, step, 0)
    out_ref[...] = out_acc[...].astype(bf16)
    again, scale = normalize(mid[...])
    mid_grad = cot_ref[...].astype(f32) + normalize_back(again, scale, back_acc[...])
    mid_grad_ref[...] = mid_grad
    rounded = mid_grad.astype(bf16)
    grad = sum(
        dot(rounded[:, o * wide : (o + 1) * wide], up[o, :, :wide], 1, 1) for o in range(seq)
    )
    merged[...] = grad.astype(bf16)
    for r in range(seq):
        for p in range(pairs):
            column = lax.bitwise_xor(s, r) * (pairs * PAIR) + p * PAIR
            grads[p * seq + r][...] = merged[:, pl.ds(pl.multiple_of(column, PAIR), PAIR)]


def middle(pairs, place, tokens, cot, heads, ups, downs, hidden):
    seq = len(heads) // pairs
    rows, width = tokens.shape
    count = ups[0].shape[0]
    dp = 2 * count
    return pl.pallas_call(
        functools.partial(middle_body, seq, pairs, count),
        in_specs=[in_smem, in_vmem, in_vmem]
        + [in_vmem] * len(heads)
        + [in_place] * (len(ups) + len(downs)),
        out_specs=[in_vmem] * (2 + len(heads)),
        out_shape=[like((rows, width)), like((rows, width), f32)]
        + [like((rows, PAIR))] * len(heads),
        scratch_shapes=[
            pltpu.VMEM((seq, width, (width + hidden) // seq), bf16),
            pltpu.VMEM((hidden, width), bf16),
            pltpu.VMEM((rows, width), bf16),
            pltpu.VMEM((rows, width), f32),
            pltpu.VMEM((rows, width), bf16),
            pltpu.VMEM((rows, width), f32),
            pltpu.VMEM((rows, width), f32),
            pltpu.SemaphoreType.DMA((seq * dp,)),
            pltpu.SemaphoreType.DMA((seq * dp,)),
        ],
        compiler_params=params(),
        cost_estimate=cost(
            8 * rows * width * hidden + 4 * rows * width * width,
            4 * width * hidden + 12 * rows * width,
            rows * hidden,
        ),
        name="middle",
    )(place, tokens, cot, *heads, *ups, *downs)


def finish_body(tokens_ref, mid_grad_ref, own_ref, got_ref, out_ref):
    normed, scale = normalize(tokens_ref[...].astype(f32))
    grad = own_ref[...] + got_ref[...].astype(f32)
    out_ref[...] = (mid_grad_ref[...] + normalize_back(normed, scale, grad)).astype(bf16)


def finish(tokens, mid_grad, own, got):
    return pl.pallas_call(
        finish_body,
        in_specs=[in_vmem] * 4,
        out_specs=in_vmem,
        out_shape=like(tokens.shape),
        compiler_params=params(),
        cost_estimate=cost(tokens.size * 20, tokens.size * 14),
        name="finish",
    )(tokens, mid_grad, own, got)


def masks(lengths, s_len):
    e0 = lengths[0]
    e1 = e0 + lengths[1]
    e2 = e1 + lengths[2]
    pos = jnp.arange(s_len, dtype=jnp.int32)
    doc = sum((pos >= e).astype(jnp.int32) for e in (e0, e1, e2))
    l = lax.broadcasted_iota(jnp.int32, (s_len, PAIR), 1)
    same = l == doc[:, None]
    mq = jnp.where((l < 4) & ~same, blocked, 0.0).astype(bf16)
    mk = jnp.where((l < 4) & same, 1.0, 0.0).astype(bf16)
    r = lax.broadcasted_iota(jnp.int32, (PREFIX_ROWS, PAIR), 0)
    lp = lax.broadcasted_iota(jnp.int32, (PREFIX_ROWS, PAIR), 1)
    pm = jnp.where((r >= PREFIX) & (lp == 3), 1.0, 0.0).astype(bf16)
    return mq, mk, pm


def reparam(embedding, inner_matrix, inner_shift, outer_matrix, outer_shift):
    hidden = jnp.tanh(
        jnp.dot(embedding, inner_matrix, precision=highest, preferred_element_type=f32)
        + inner_shift
    )
    return (
        jnp.dot(hidden, outer_matrix, precision=highest, preferred_element_type=f32) + outer_shift
    )


def halvings(count):
    steps = []
    while count > 1:
        count //= 2
        steps.append(count)
    return steps


def swap(value, axis, size, mask):
    return lax.ppermute(value, axis, [(i, i ^ mask) for i in range(size)])


def gather_dp(piece, dp):
    far = dp // 2
    line = [piece] + [
        lax.ppermute(piece, "dp", [(i, (i + 2 * k) % dp) for i in range(dp)]) for k in range(1, far)
    ]
    line = jnp.stack(line)
    return [line, swap(line, "dp", dp, 1)]


def places(dp):
    me = lax.axis_index("dp")
    far = dp // 2
    row, side = me // 2, lax.rem(me, 2)
    steps = lax.rem(row - jnp.arange(far, dtype=jnp.int32) + far, far) * 2
    head = jnp.reshape(lax.axis_index("seq"), (1,))
    return jnp.concatenate([head, steps + side, steps + 1 - side]).astype(jnp.int32)


def spread_seq(values, seq):
    held = {0: values}
    for mask in halvings(seq):
        for r in list(held):
            held[r ^ mask] = [swap(v, "seq", seq, mask) for v in held[r]]
    return [held[r] for r in range(seq)]


def exchange_seq(pieces, seq):
    return [pieces[0]] + [swap(pieces[r], "seq", seq, r) for r in range(1, seq)]


def shards(seq, dp, tokens, lengths, attend_weight, output_weight, expand_weight, shrink_weight,
           prefix_embed, inner_weight, inner_bias, outer_weight, outer_bias, cotangent):
    s = lax.axis_index("seq")
    rows, width = tokens.shape[1:]
    s_len = rows * seq
    pairs = width // seq // PAIR
    token_rows = tokens[0]
    place = places(dp)

    normed = normalize(token_rows.astype(f32))[0].astype(bf16)
    normed = [v[0] for v in spread_seq([normed], seq)]
    attend_pairs = [gather_dp(w, dp) for w in cut_attend(seq, pairs, place, attend_weight)]
    up, down = cut_rest(seq, place, output_weight, expand_weight, shrink_weight)
    ups = [w for pair in spread_seq(gather_dp(up, dp), seq) for w in pair]
    down = gather_dp(down, dp)
    downs = down + [swap(w, "seq", seq, 1) for w in down]

    prefix_kv, reparam_back = jax.vjp(
        reparam, prefix_embed, inner_weight, inner_bias, outer_weight, outer_bias
    )
    padded = jnp.pad(prefix_kv.astype(bf16), ((0, PREFIX_ROWS - PREFIX), (0, 0)))
    prefix_mine = lax.dynamic_index_in_dim(
        padded.reshape(PREFIX_ROWS, 2, seq, pairs, PAIR), s, 2, keepdims=False
    )
    prefix_pairs = [(prefix_mine[:, 0, p], prefix_mine[:, 1, p]) for p in range(pairs)]
    mask_q, mask_k, mask_p = masks(lengths[0], s_len)

    saved, heads = [], []
    for p in range(pairs):
        qkv, stat, weight, *outs = attend_forward(
            place, normed, *attend_pairs[p], *prefix_pairs[p], mask_q, mask_k, mask_p
        )
        saved.append((qkv, stat, weight, outs))
        heads += exchange_seq(outs, seq)
    outputs, mid_grad, *out_grads = middle(
        pairs, place, token_rows, cotangent[0], heads, ups, downs, expand_weight.shape[1]
    )
    grads, prefix_terms = [], []
    for p in range(pairs):
        qkv, stat, weight, outs = saved[p]
        got = exchange_seq(out_grads[p * seq : (p + 1) * seq], seq)
        *parts, prefix_part = attend_backward(
            place, qkv, *prefix_pairs[p], stat, mask_k, mask_p, outs, got
        )
        grads.append(parts)
        prefix_terms.append(prefix_part)

    blocks = {
        r: sum(dot(grads[p][r], saved[p][2], 1, 1) for p in range(pairs)) for r in range(seq)
    }
    got = None
    for mask in reversed(halvings(seq)):
        keep = {}
        for r in [r for r in blocks if not r & mask]:
            got = swap(blocks[r ^ mask].astype(bf16), "seq", seq, mask)
            keep[r] = blocks[r] if len(blocks) == 2 else blocks[r] + got.astype(f32)
        blocks = keep
    input_grad = finish(token_rows, mid_grad, blocks[0], got)

    prefix_sum = jnp.stack(prefix_terms, axis=2)
    for mask in halvings(dp):
        prefix_sum = prefix_sum + swap(prefix_sum, "dp", dp, mask)
    prefix_grad = jnp.zeros((2, PREFIX_ROWS, seq, pairs, PAIR), f32)
    for r, (got,) in enumerate(spread_seq([prefix_sum], seq)):
        prefix_grad = lax.dynamic_update_slice(prefix_grad, got[:, :, None], (0, 0, s ^ r, 0, 0))
    prefix_grad = prefix_grad[:, :PREFIX].reshape(2, PREFIX, width)
    back = reparam_back(jnp.concatenate([prefix_grad[0], prefix_grad[1]], axis=1))
    return (outputs[None], input_grad[None], *back, prefix_kv)


def solution(mesh):
    placed = (
        P("dp", "seq", None),
        P("dp", None),
        P("dp", None),
        P("dp", None),
        P("dp", None),
        P("dp", None),
        P(),
        P(),
        P(),
        P(),
        P(),
        P("dp", "seq", None),
    )
    return jax.shard_map(
        functools.partial(shards, mesh.shape["seq"], mesh.shape["dp"]),
        mesh=mesh,
        in_specs=placed,
        out_specs=(P("dp", "seq", None), P("dp", "seq", None), P(), P(), P(), P(), P(), P()),
        check_vma=False,
    )
```

time: 456 us -> 417 us (0.914)
  local copies, waits for them, and re-layouts: 95.1 us -> 10.3 us
  matrix products: 105 us -> 35.3 us
  Pallas kernels: 46.5 us -> 108 us
  waiting for transfers between devices: 107 us -> 155 us
  starting transfers between devices: 69.7 us -> 82.1 us
    pallas_call x4 -> x8, Pallas kernels: 46.5 us -> 108 us  [the longest x2 36.2 us: attend_backward(): pl.pallas_call(functools.partial(backward_body, seq, bq, bk), in_specs=[i...]
    dynamic_update_slice x53 -> x4, local copies, waits for them, and re-layouts: 47.3 us -> 0.16 us  [shards(): lax.dynamic_update_slice(prefix_grad, got[:, :, None], (0, 0, s ^ r, 0, 0))]
    dot_general x11 -> x0, matrix products: 41.5 us -> none  [the longest x4 17.9 us: shards(): jnp.dot(activated.astype(bf16), down, preferred_element_type=f32)]
    ppermute x15 -> x12, waiting for transfers between devices: 2.78 us -> 42.3 us  [gather_dp(): lax.ppermute(piece, 'dp', [(i, (i + 2 * k) % dp) for i in range(dp)])]
    dot_general x7 -> x8, matrix products: 42.5 us -> 14.4 us  [dot(): lax.dot_general(a, b, (((ca,), (cb,)), ((), ())), preferred_element_type=...]
    ppermute x15 -> x12, starting transfers between devices: 25.3 us -> 45.9 us  [gather_dp(): lax.ppermute(piece, 'dp', [(i, (i + 2 * k) % dp) for i in range(dp)])]
    another operation x14 -> x0, local copies, waits for them, and re-layouts: 12.3 us -> none
    broadcast_in_dim x11 -> x0, local copies, waits for them, and re-layouts: 12.1 us -> none  [the longest x6 9.61 us: gather_dp(): line = put(line, got[None], (lax.rem(mine - k + far, far),) + zero)]
  transfers between devices with their start and end apart: 53 -> 48, of which waited for: 17 -> 22; matrix products, arithmetic and copies ran while one was open for 42% -> 14% of each run, Pallas kernels for 4% -> 12%
where the time goes in v2:
time: 417 us; the launch traced here: 411 us
  waiting for transfers between devices  155 us (37%)
  Pallas kernels  108 us (26%)
  starting transfers between devices  82.1 us (20%)
  matrix products  35.3 us (8%)
  other arithmetic  17.2 us (4%)
  local copies, waits for them, and re-layouts  10.3 us (2%)
    ppermute x36, waiting for transfers between devices, swap(): return lax.ppermute(value, axis, [(i, i ^ mask) for i in range(size)])  112 us
    ppermute x12, starting transfers between devices, gather_dp(): lax.ppermute(piece, 'dp', [(i, (i + 2 * k) % dp) for i in range(dp)])  45.9 us
    ppermute x12, waiting for transfers between devices, gather_dp(): lax.ppermute(piece, 'dp', [(i, (i + 2 * k) % dp) for i in range(dp)])  42.3 us
    pallas_call x2, Pallas kernels, attend_backward(): pl.pallas_call(functools.partial(backward_body, seq, bq, bk), in_specs=[i...  36.2 us
    ppermute x36, starting transfers between devices, swap(): return lax.ppermute(value, axis, [(i, i ^ mask) for i in range(size)])  36.1 us
    pallas_call x1, Pallas kernels, middle(): pl.pallas_call(functools.partial(middle_body, seq, pairs, count), in_spec...  33.9 us
    pallas_call x2, Pallas kernels, attend_forward(): pl.pallas_call(functools.partial(forward_body, seq, bq, bk), in_specs=[in...  28.4 us
    dot_general x8, matrix products, dot(): lax.dot_general(a, b, (((ca,), (cb,)), ((), ())), preferred_element_type=...  14.4 us
  transfers between devices with their start and end apart: 48, of which 22 were waited for; matrix products, arithmetic and copies ran while one was open for 14% of the time, Pallas kernels for 12%

profile of v2, /device:TPU:0, one launch (start us, length us, event | category | flops | bytes accessed | tf_op | source)
XLA Modules:
  0.0 411.2 jit_solution(1292425273578374932)
XLA Ops:
  1.3 1.9 cut_attend.1
  3.2 3.0 collective-permute-start.10
  6.2 2.6 collective-permute-start.11
  8.8 2.6 cut_rest.1
  11.4 1.8 collective-permute-start.28
  13.3 1.9 collective-permute-start.29
  17.0 2.8 fusion.13
  19.8 1.3 fusion.3.refs_0_
  21.1 1.5 collective-permute-start.1
  22.6 14.0 %collective-permute-done.11 = bf16[128,384]{1,0:T(8,128)(2,1)S(1)} collective-permute-done((bf16[128,384]{1,0:T(8,128)(2,1)}, bf16[128,384]{1,0:T(8,128)(2,1)S(1)}, u32[]{:S(2)}, u32[]{:S(2)}) %collective-permute-start.11) | collective-permute-done | bytes 98336 | tf_op jit(solution)/shard_map/ppermute | solution.py:548
  36.6 14.7 %collective-permute-done.12 = bf16[128,384]{1,0:T(8,128)(2,1)S(1)} collective-permute-done((bf16[128,384]{1,0:T(8,128)(2,1)S(1)}, bf16[128,384]{1,0:T(8,128)(2,1)S(1)}, u32[]{:S(2)}, u32[]{:S(2)}) %collective-permute-start.12) | collective-permute-done | bytes 98336 | tf_op jit(solution)/shard_map/ppermute | solution.py:548
  51.3 19.0 %collective-permute-start.17 = (bf16[128,1280]{1,0:T(8,128)(2,1)S(1)}, bf16[128,1280]{1,0:T(8,128)(2,1)S(1)}, u32[]{:S(2)}, u32[]{:S(2)}) collective-permute-start(bf16[128,1280]{1,0:T(8,128)(2,1)S(1)} %copy-done.19), channel_id=1, source_target_pairs={{0,2},{1,3},{2,4},{3,5},{4,6},{5,7},{6,0},{7,1},{8,10},{9,11},{10,... | collective-permute-start | bytes 983048 | tf_op jit(solution)/shard_map/ppermute | solution.py:548
  70.2 2.4 collective-permute-start.19
  74.9 3.1 pad_maximum_fusion.refs_18_
  78.3 2.5 collective-permute-start.3
  80.7 7.5 %collective-permute-done.18 = bf16[128,1280]{1,0:T(8,128)(2,1)S(1)} collective-permute-done((bf16[128,1280]{1,0:T(8,128)(2,1)S(1)}, bf16[128,1280]{1,0:T(8,128)(2,1)S(1)}, u32[]{:S(2)}, u32[]{:S(2)}) %collective-permute-start.18) | collective-permute-done | bytes 327712 | tf_op jit(solution)/shard_map/ppermute | solution.py:548
  88.8 3.6 collective-permute-done.19
  92.3 1.5 collective-permute-start.30
  93.9 1.4 pad_maximum_fusion.1.refs_10_
  95.3 12.1 %collective-permute-start.5 = (bf16[128,384]{1,0:T(8,128)(2,1)S(1)}, bf16[128,384]{1,0:T(8,128)(2,1)S(1)}, u32[]{:S(2)}, u32[]{:S(2)}) collective-permute-start(bf16[128,384]{1,0:T(8,128)(2,1)S(1)} %copy-done.28), channel_id=1, source_target_pairs={{0,6},{1,7},{2,0},{3,1},{4,2},{5,3},{6,4},{7,5},{8,14},{9,15},{10,... | collective-permute-start | bytes 294920 | tf_op jit(solution)/shard_map/ppermute | solution.py:548
  108.2 2.3 collective-permute-done.5
  113.2 62.6 %collective-permute-done.13.refs_5_ = bf16[4,128,384]{2,1,0:T(8,128)(2,1)S(1)} collective-permute-done((bf16[4,128,384]{2,1,0:T(8,128)(2,1)S(1)}, bf16[4,128,384]{2,1,0:T(8,128)(2,1)S(1)}, u32[]{:S(2)}, u32[]{:S(2)}) %collective-permute-start.13) | collective-permute-done | bytes 393248 | tf_op jit(solution)/shard_map/ppermute | solution.py:542
  175.8 1.5 collective-permute-start.23
  180.0 1.5 select_convert_fusion
  182.6 1.6 collective-permute-start.6
  184.8 14.1 %attend_forward.3 = (bf16[2048,384]{1,0:T(8,128)(2,1)}, bf16[2048,128]{1,0:T(8,128)(2,1)}, bf16[1024,384]{1,0:T(8,128)(2,1)}, bf16[512,128]{1,0:T(8,128)(2,1)}, ...) custom-call(s32[9]{0:T(128)} %pad_add_fusion.place, ...), custom_call_target="tpu_custom_call" | custom-call | flops 5905580032 | bytes 6291456 | tf_op jit(solution)/shard_map/attend_forward/pallas_call | solution.py:211
  199.0 8.6 %collective-permute-done.23.refs_14_ = bf16[4,128,1280]{2,1,0:T(8,128)(2,1)} collective-permute-done((bf16[4,128,1280]{2,1,0:T(8,128)(2,1)S(1)}, bf16[4,128,1280]{2,1,0:T(8,128)(2,1)}, u32[]{:S(2)}, u32[]{:S(2)}) %collective-permute-start.23) | collective-permute-done | bytes 1310752 | tf_op jit(solution)/shard_map/ppermute | solution.py:542
  207.6 1.5 collective-permute-start.15
  209.4 14.3 %attend_forward.2 = (bf16[2048,384]{1,0:T(8,128)(2,1)}, bf16[2048,128]{1,0:T(8,128)(2,1)}, bf16[1024,384]{1,0:T(8,128)(2,1)}, bf16[512,128]{1,0:T(8,128)(2,1)}, ...) custom-call(s32[9]{0:T(128)} %pad_add_fusion.place, ...), custom_call_target="tpu_custom_call" | custom-call | flops 5905580032 | bytes 6291456 | tf_op jit(solution)/shard_map/attend_forward/pallas_call | solution.py:211
  224.2 12.9 %collective-permute-done.15.refs_8_ = bf16[512,128]{1,0:T(8,128)(2,1)S(1)} collective-permute-done((bf16[512,128]{1,0:T(8,128)(2,1)}, bf16[512,128]{1,0:T(8,128)(2,1)S(1)}, u32[]{:S(2)}, u32[]{:S(2)}) %collective-permute-start.15) | collective-permute-done | bytes 131104 | tf_op jit(solution)/shard_map/ppermute | solution.py:542
  238.7 1.2 collective-permute-start.9
  239.9 4.2 %collective-permute-done.8.refs_4_ = bf16[512,128]{1,0:T(8,128)(2,1)S(1)} collective-permute-done((bf16[512,128]{1,0:T(8,128)(2,1)}, bf16[512,128]{1,0:T(8,128)(2,1)S(1)}, u32[]{:S(2)}, u32[]{:S(2)}) %collective-permute-start.8) | collective-permute-done | bytes 131104 | tf_op jit(solution)/shard_map/ppermute | solution.py:542
  244.1 2.5 collective-permute-done.9.refs_5_
  247.3 2.5 collective-permute-done.25.refs_16_
  249.8 1.9 collective-permute-done.26.refs_17_
  253.4 33.9 %middle.1 = (bf16[512,1024]{1,0:T(8,128)(2,1)}, f32[512,1024]{1,0:T(8,128)}, bf16[512,128]{1,0:T(8,128)(2,1)}, bf16[512,128]{1,0:T(8,128)(2,1)}, bf16[512,128]{1...) custom-call(s32[9]{0:T(128)} %pad_add_fusion.place, ...), custom_call_target="tpu_custom_call" | custom-call | flops 19327352832 | bytes 23068672 | tf_op jit(solution)/shard_map/middle/pallas_call | solution.py:460
  287.5 1.5 collective-permute-start.34
  289.7 1.5 collective-permute-start.37
  291.2 2.9 collective-permute-done.34.refs_12_
  294.0 1.9 collective-permute-done.35.refs_13_
  296.6 18.1 %attend_backward.2 = (bf16[512,384]{1,0:T(8,128)(2,1)}, bf16[512,384]{1,0:T(8,128)(2,1)}, bf16[512,384]{1,0:T(8,128)(2,1)}, bf16[512,384]{1,0:T(8,128)(2,1)}, f32[2,16,128]{2,1,0:T(8,128)}) custom-call(s32[9]{0:T(128)} %pad_add_fusion.place, bf16[2048,384]{1,0:T(8,128)(2,1)} %get-tuple-element.60.refs_0_, ...), custom_call_target="tpu_custom_call" | custom-call | flops 10737418240 | bytes 6291456 | tf_op jit(solution)/shard_map/attend_backward/pallas_call | solution.py:334
  315.4 18.1 %attend_backward.3 = (bf16[512,384]{1,0:T(8,128)(2,1)}, bf16[512,384]{1,0:T(8,128)(2,1)}, bf16[512,384]{1,0:T(8,128)(2,1)}, bf16[512,384]{1,0:T(8,128)(2,1)}, f32[2,16,128]{2,1,0:T(8,128)}) custom-call(s32[9]{0:T(128)} %pad_add_fusion.place, bf16[2048,384]{1,0:T(8,128)(2,1)} %get-tuple-element.68.refs_0_, ...), custom_call_target="tpu_custom_call" | custom-call | flops 10737418240 | bytes 6291456 | tf_op jit(solution)/shard_map/attend_backward/pallas_call | solution.py:334
  334.4 5.7 %collective-permute-start.42 = (f32[2,16,2,128]{3,1,0,2:T(8,128)S(1)}, f32[2,16,2,128]{3,1,0,2:T(8,128)S(1)}, u32[]{:S(2)}, u32[]{:S(2)}) collective-permute-start(f32[2,16,2,128]{3,1,0,2:T(8,128)S(1)} %pad_maximum_fusion.4), channel_id=1, source_target_pairs={{0,4},{1,5},{2,6},{3,7},{4,0},{5,1},{6,2},{7,3},{8,12},{9,13},{10,... | collective-permute-start | bytes 98312 | tf_op jit(solution)/shard_map/ppermute | solution.py:542
  340.1 3.1 fusion.19
  344.3 1.7 add_convert_fusion.1
  347.3 1.7 add_convert_fusion.2
  349.0 2.1 fusion.18
  351.1 7.8 %collective-permute-start.43 = (f32[2,16,2,128]{3,1,0,2:T(8,128)S(1)}, f32[2,16,2,128]{3,1,0,2:T(8,128)S(1)}, u32[]{:S(2)}, u32[]{:S(2)}) collective-permute-start(f32[2,16,2,128]{3,1,0,2:T(8,128)S(1)} %fusion.10), channel_id=1, source_target_pairs={{0,2},{1,3},{2,0},{3,1},{4,6},{5,7},{6,4},{7,5},{8,10},{9,11},{10,... | collective-permute-start | bytes 98312 | tf_op jit(solution)/shard_map/ppermute | solution.py:542
  358.9 2.3 fusion.16
  361.2 1.6 collective-permute-start.44
  362.8 2.1 fusion.15
  365.5 1.5 collective-permute-start.46
  367.6 1.8 collective-permute-done.46
  369.4 1.2 collective-permute-done.47
  370.8 6.4 %fusion.14 = (f32[512]{0:T(512)}, f32[10,512]{1,0:T(8,128)S(1)}) fusion(f32[10,512]{1,0:T(8,128)S(1)} %fusion.4, f32[10,2048]{1,0:T(8,128)S(1)} %constant_dynamic-update-slice_fusion, f32[512,2048]{1,0:T(8,128)} %param.21), kind=kOutput, calls=%fused_computation.59 | convolution fusion | flops 125854208 | bytes 4319232 | tf_op jit(solution)/shard_map/transpose(jvp())/dot_general | solution.py:529
  377.2 2.9 add_convert_fusion
  380.1 1.5 collective-permute-start.41
  381.6 3.2 convolution_bitcast_fusion
  385.4 2.9 copy.27
  388.3 2.5 fusion.21
  390.7 5.0 %fusion.22 = f32[512,2048]{1,0:T(8,128)} fusion(f32[10,512]{1,0:T(8,128)S(1)} %fusion.4, f32[10,2048]{1,0:T(8,128)S(1)} %constant_dynamic-update-slice_fusion), kind=kOutput, calls=%fused_computation.67 | convolution fusion | flops 125829120 | bytes 4296704 | tf_op jit(solution)/shard_map/transpose(jvp())/dot_general | solution.py:529
  395.8 2.0 convert_add_fusion.own_ref
  397.7 7.9 %collective-permute-done.41.got_ref = bf16[512,1024]{1,0:T(8,128)(2,1)} collective-permute-done((bf16[512,1024]{1,0:T(8,128)(2,1)}, bf16[512,1024]{1,0:T(8,128)(2,1)}, u32[]{:S(2)}, u32[]{:S(2)}) %collective-permute-start.41) | collective-permute-done | bytes 1048608 | tf_op jit(solution)/shard_map/ppermute | solution.py:542
  405.6 5.2 %finish.1 = bf16[512,1024]{1,0:T(8,128)(2,1)} custom-call(bf16[512,1024]{1,0:T(8,128)(2,1)} %bitcast.75, f32[512,1024]{1,0:T(8,128)} %get-tuple-element.59.mid_grad_ref, f32[512,1024]{1,0:T(8,128)} %convert_add_fusion.own_ref, bf16[512,1024]{1,0:T(8,128)(2,1)} %collective-permute-done.41.got_ref), custom_call_target="tpu_custom_call" | custom-call | flops 10485760 | bytes 7340032 | tf_op jit(solution)/shard_map/finish/pallas_call | solution.py:496
  (223 shorter events, 23.7 us)
Async XLA Ops:
  3.2 17.9 %collective-permute-start.10 = (bf16[128,384]{1,0:T(8,128)(2,1)}, bf16[128,384]{1,0:T(8,128)(2,1)S(1)}, u32[]{:S(2)}, u32[]{:S(2)}) collective-permute-start(bf16[128,384]{1,0:T(8,128)(2,1)} %get-tuple-element.51), channel_id=1, source_target_pairs={{0,2},{1,3},{2,4},{3,5},{4,6},{5,7},{6,0},{7,1},{8,10},{9,11},{10,... | collective-permute-start | bytes 294920 | tf_op jit(solution)/shard_map/ppermute | solution.py:548
  6.2 30.4 %collective-permute-start.11 = (bf16[128,384]{1,0:T(8,128)(2,1)}, bf16[128,384]{1,0:T(8,128)(2,1)S(1)}, u32[]{:S(2)}, u32[]{:S(2)}) collective-permute-start(bf16[128,384]{1,0:T(8,128)(2,1)} %get-tuple-element.51), channel_id=1, source_target_pairs={{0,4},{1,5},{2,6},{3,7},{4,0},{5,1},{6,2},{7,3},{8,12},{9,13},{10,... | collective-permute-start | bytes 294920 | tf_op jit(solution)/shard_map/ppermute | solution.py:548
  11.4 39.9 %collective-permute-start.27 = (bf16[256,1024]{1,0:T(8,128)(2,1)}, bf16[256,1024]{1,0:T(8,128)(2,1)}, u32[]{:S(2)}, u32[]{:S(2)}) collective-permute-start(bf16[256,1024]{1,0:T(8,128)(2,1)} %get-tuple-element.57), channel_id=1, source_target_pairs={{0,2},{1,3},{2,4},{3,5},{4,6},{5,7},{6,0},{7,1},{8,10},{9,11},{10,... | collective-permute-start | bytes 1572872 | tf_op jit(solution)/shard_map/ppermute | solution.py:548
  11.4 58.8 %collective-permute-start.28 = (bf16[256,1024]{1,0:T(8,128)(2,1)}, bf16[256,1024]{1,0:T(8,128)(2,1)}, u32[]{:S(2)}, u32[]{:S(2)}) collective-permute-start(bf16[256,1024]{1,0:T(8,128)(2,1)} %get-tuple-element.57), channel_id=1, source_target_pairs={{0,4},{1,5},{2,6},{3,7},{4,0},{5,1},{6,2},{7,3},{8,12},{9,13},{10,... | collective-permute-start | bytes 1572872 | tf_op jit(solution)/shard_map/ppermute | solution.py:548
  13.3 56.9 %collective-permute-start.29 = (bf16[256,1024]{1,0:T(8,128)(2,1)}, bf16[256,1024]{1,0:T(8,128)(2,1)}, u32[]{:S(2)}, u32[]{:S(2)}) collective-permute-start(bf16[256,1024]{1,0:T(8,128)(2,1)} %get-tuple-element.57), channel_id=1, source_target_pairs={{0,6},{1,7},{2,0},{3,1},{4,2},{5,3},{6,4},{7,5},{8,14},{9,15},{10,... | collective-permute-start | bytes 1572872 | tf_op jit(solution)/shard_map/ppermute | solution.py:548
  19.8 31.5 %copy-start.19 = (bf16[128,1280]{1,0:T(8,128)(2,1)S(1)}, bf16[128,1280]{1,0:T(8,128)(2,1)}, u32[]{:S(2)}) copy-start(bf16[128,1280]{1,0:T(8,128)(2,1)} %get-tuple-element.56) | copy-start | bytes 983044
  21.1 51.6 %copy-start.32 = (bf16[128,384]{1,0:T(8,128)(2,1)}, bf16[128,384]{1,0:T(8,128)(2,1)S(1)}, u32[]{:S(2)}) copy-start(bf16[128,384]{1,0:T(8,128)(2,1)S(1)} %collective-permute-done.10) | copy-start | bytes 294916
  21.1 90.9 %collective-permute-start.1 = (bf16[512,1024]{1,0:T(8,128)(2,1)}, bf16[512,1024]{1,0:T(8,128)(2,1)}, u32[]{:S(2)}, u32[]{:S(2)}) collective-permute-start(bf16[512,1024]{1,0:T(8,128)(2,1)} %fusion.3.refs_0_), channel_id=1, source_target_pairs={{0,16},{8,24},{16,0},{24,8},{1,17},{9,25},{17,1},{25,9},{2,18},{10... | collective-permute-start | bytes 3145736 | tf_op jit(solution)/shard_map/ppermute | solution.py:542
  36.5 36.1 %copy-start.34 = (bf16[128,384]{1,0:T(8,128)(2,1)}, bf16[128,384]{1,0:T(8,128)(2,1)S(1)}, u32[]{:S(2)}) copy-start(bf16[128,384]{1,0:T(8,128)(2,1)S(1)} %collective-permute-done.11) | copy-start | bytes 294916
  36.5 14.7 %collective-permute-start.12 = (bf16[128,384]{1,0:T(8,128)(2,1)S(1)}, bf16[128,384]{1,0:T(8,128)(2,1)S(1)}, u32[]{:S(2)}, u32[]{:S(2)}) collective-permute-start(bf16[128,384]{1,0:T(8,128)(2,1)S(1)} %copy-done.30), channel_id=1, source_target_pairs={{0,6},{1,7},{2,0},{3,1},{4,2},{5,3},{6,4},{7,5},{8,14},{9,15},{10,... | collective-permute-start | bytes 294920 | tf_op jit(solution)/shard_map/ppermute | solution.py:548
  51.2 21.4 %copy-start.37 = (bf16[128,384]{1,0:T(8,128)(2,1)}, bf16[128,384]{1,0:T(8,128)(2,1)S(1)}, u32[]{:S(2)}) copy-start(bf16[128,384]{1,0:T(8,128)(2,1)S(1)} %collective-permute-done.12) | copy-start | bytes 294916
  51.2 126.1 %collective-permute-start = (bf16[512,1024]{1,0:T(8,128)(2,1)}, bf16[512,1024]{1,0:T(8,128)(2,1)}, u32[]{:S(2)}, u32[]{:S(2)}) collective-permute-start(bf16[512,1024]{1,0:T(8,128)(2,1)} %fusion.3.refs_0_), channel_id=1, source_target_pairs={{0,8},{8,0},{16,24},{24,16},{1,9},{9,1},{17,25},{25,17},{2,10},{10... | collective-permute-start | bytes 3145736 | tf_op jit(solution)/shard_map/ppermute | solution.py:542
  51.3 27.0 %collective-permute-start.17 = (bf16[128,1280]{1,0:T(8,128)(2,1)S(1)}, bf16[128,1280]{1,0:T(8,128)(2,1)S(1)}, u32[]{:S(2)}, u32[]{:S(2)}) collective-permute-start(bf16[128,1280]{1,0:T(8,128)(2,1)S(1)} %copy-done.19), channel_id=1, source_target_pairs={{0,2},{1,3},{2,4},{3,5},{4,6},{5,7},{6,0},{7,1},{8,10},{9,11},{10,... | collective-permute-start | bytes 983048 | tf_op jit(solution)/shard_map/ppermute | solution.py:548
  70.2 18.0 %collective-permute-start.18 = (bf16[128,1280]{1,0:T(8,128)(2,1)S(1)}, bf16[128,1280]{1,0:T(8,128)(2,1)S(1)}, u32[]{:S(2)}, u32[]{:S(2)}) collective-permute-start(bf16[128,1280]{1,0:T(8,128)(2,1)S(1)} %copy-done.19), channel_id=1, source_target_pairs={{0,4},{1,5},{2,6},{3,7},{4,0},{5,1},{6,2},{7,3},{8,12},{9,13},{10,... | collective-permute-start | bytes 983048 | tf_op jit(solution)/shard_map/ppermute | solution.py:548
  70.2 22.1 %collective-permute-start.19 = (bf16[128,1280]{1,0:T(8,128)(2,1)S(1)}, bf16[128,1280]{1,0:T(8,128)(2,1)S(1)}, u32[]{:S(2)}, u32[]{:S(2)}) collective-permute-start(bf16[128,1280]{1,0:T(8,128)(2,1)S(1)} %copy-done.19), channel_id=1, source_target_pairs={{0,6},{1,7},{2,0},{3,1},{4,2},{5,3},{6,4},{7,5},{8,14},{9,15},{10,... | collective-permute-start | bytes 983048 | tf_op jit(solution)/shard_map/ppermute | solution.py:548
  78.0 30.1 %copy-start.31 = (bf16[128,384]{1,0:T(8,128)(2,1)S(1)}, bf16[128,384]{1,0:T(8,128)(2,1)}, u32[]{:S(2)}) copy-start(bf16[128,384]{1,0:T(8,128)(2,1)} %get-tuple-element.51) | copy-start | bytes 294916
  78.0 30.1 %copy-start.33 = (bf16[128,384]{1,0:T(8,128)(2,1)S(1)}, bf16[128,384]{1,0:T(8,128)(2,1)}, u32[]{:S(2)}) copy-start(bf16[128,384]{1,0:T(8,128)(2,1)} %copy-done.32) | copy-start | bytes 294916
  78.0 30.1 %copy-start.35 = (bf16[128,384]{1,0:T(8,128)(2,1)S(1)}, bf16[128,384]{1,0:T(8,128)(2,1)}, u32[]{:S(2)}) copy-start(bf16[128,384]{1,0:T(8,128)(2,1)} %copy-done.34) | copy-start | bytes 294916
  78.0 30.1 %copy-start.38 = (bf16[128,384]{1,0:T(8,128)(2,1)S(1)}, bf16[128,384]{1,0:T(8,128)(2,1)}, u32[]{:S(2)}) copy-start(bf16[128,384]{1,0:T(8,128)(2,1)} %copy-done.37) | copy-start | bytes 294916
  78.0 34.0 %copy-start.42 = (s32[1,3]{1,0:T(1,128)S(1)}, s32[1,3]{1,0:T(1,128)}, u32[]{:S(2)}) copy-start(s32[1,3]{1,0:T(1,128)} %param.13) | copy-start | bytes 40
  78.3 17.0 %collective-permute-start.3 = (bf16[128,384]{1,0:T(8,128)(2,1)S(1)}, bf16[128,384]{1,0:T(8,128)(2,1)S(1)}, u32[]{:S(2)}, u32[]{:S(2)}) collective-permute-start(bf16[128,384]{1,0:T(8,128)(2,1)S(1)} %copy-done.28), channel_id=1, source_target_pairs={{0,2},{1,3},{2,4},{3,5},{4,6},{5,7},{6,0},{7,1},{8,10},{9,11},{10,... | collective-permute-start | bytes 294920 | tf_op jit(solution)/shard_map/ppermute | solution.py:548
  88.3 19.1 %collective-permute-start.4 = (bf16[128,384]{1,0:T(8,128)(2,1)S(1)}, bf16[128,384]{1,0:T(8,128)(2,1)S(1)}, u32[]{:S(2)}, u32[]{:S(2)}) collective-permute-start(bf16[128,384]{1,0:T(8,128)(2,1)S(1)} %copy-done.28), channel_id=1, source_target_pairs={{0,4},{1,5},{2,6},{3,7},{4,0},{5,1},{6,2},{7,3},{8,12},{9,13},{10,... | collective-permute-start | bytes 294920 | tf_op jit(solution)/shard_map/ppermute | solution.py:548
  92.3 116.8 %collective-permute-start.30 = (bf16[4,256,1024]{2,1,0:T(8,128)(2,1)}, bf16[4,256,1024]{2,1,0:T(8,128)(2,1)}, u32[]{:S(2)}, u32[]{:S(2)}) collective-permute-start(bf16[4,256,1024]{2,1,0:T(8,128)(2,1)} %pad_maximum_fusion.refs_18_), channel_id=1, source_target_pairs={{0,1},{1,0},{2,3},{3,2},{4,5},{5,4},{6,7},{7,6},{8,9},{9,8},{10,11... | collective-permute-start | bytes 6291464 | tf_op jit(solution)/shard_map/ppermute | solution.py:542
  93.9 87.6 %copy-start.29 = (bf16[128,384]{1,0:T(8,128)(2,1)S(1)}, bf16[128,384]{1,0:T(8,128)(2,1)}, u32[]{:S(2)}) copy-start(bf16[128,384]{1,0:T(8,128)(2,1)} %get-tuple-element.46) | copy-start | bytes 294916
  95.3 103.7 %copy-start.9 = (bf16[4,128,1280]{2,1,0:T(8,128)(2,1)}, bf16[4,128,1280]{2,1,0:T(8,128)(2,1)S(1)}, u32[]{:S(2)}) copy-start(bf16[4,128,1280]{2,1,0:T(8,128)(2,1)S(1)} %pad_maximum_fusion.1.refs_10_) | copy-start | bytes 3932164
  95.3 82.0 %copy-start.36 = (bf16[128,384]{1,0:T(8,128)(2,1)}, bf16[128,384]{1,0:T(8,128)(2,1)S(1)}, u32[]{:S(2)}) copy-start(bf16[128,384]{1,0:T(8,128)(2,1)S(1)} %collective-permute-done.3) | copy-start | bytes 294916
  95.3 15.2 %collective-permute-start.5 = (bf16[128,384]{1,0:T(8,128)(2,1)S(1)}, bf16[128,384]{1,0:T(8,128)(2,1)S(1)}, u32[]{:S(2)}, u32[]{:S(2)}) collective-permute-start(bf16[128,384]{1,0:T(8,128)(2,1)S(1)} %copy-done.28), channel_id=1, source_target_pairs={{0,6},{1,7},{2,0},{3,1},{4,2},{5,3},{6,4},{7,5},{8,14},{9,15},{10,... | collective-permute-start | bytes 294920 | tf_op jit(solution)/shard_map/ppermute | solution.py:548
  107.4 70.0 %copy-start.39 = (bf16[128,384]{1,0:T(8,128)(2,1)}, bf16[128,384]{1,0:T(8,128)(2,1)S(1)}, u32[]{:S(2)}) copy-start(bf16[128,384]{1,0:T(8,128)(2,1)S(1)} %collective-permute-done.4) | copy-start | bytes 294916
  107.4 75.1 %collective-permute-start.20 = (bf16[4,128,1280]{2,1,0:T(8,128)(2,1)S(1)}, bf16[4,128,1280]{2,1,0:T(8,128)(2,1)}, u32[]{:S(2)}, u32[]{:S(2)}) collective-permute-start(bf16[4,128,1280]{2,1,0:T(8,128)(2,1)S(1)} %pad_maximum_fusion.1.refs_10_), channel_id=1, source_target_pairs={{0,1},{1,0},{2,3},{3,2},{4,5},{5,4},{6,7},{7,6},{8,9},{9,8},{10,11... | collective-permute-start | bytes 3932168 | tf_op jit(solution)/shard_map/ppermute | solution.py:542
  108.2 69.1 %copy-start.17 = (bf16[4,128,384]{2,1,0:T(8,128)(2,1)}, bf16[4,128,384]{2,1,0:T(8,128)(2,1)S(1)}, u32[]{:S(2)}) copy-start(bf16[4,128,384]{2,1,0:T(8,128)(2,1)S(1)} %pad_maximum_fusion.3.refs_4_) | copy-start | bytes 1179652
  110.5 66.9 %copy-start.40 = (bf16[128,384]{1,0:T(8,128)(2,1)}, bf16[128,384]{1,0:T(8,128)(2,1)S(1)}, u32[]{:S(2)}) copy-start(bf16[128,384]{1,0:T(8,128)(2,1)S(1)} %collective-permute-done.5) | copy-start | bytes 294916
  110.5 65.3 %collective-permute-start.13 = (bf16[4,128,384]{2,1,0:T(8,128)(2,1)S(1)}, bf16[4,128,384]{2,1,0:T(8,128)(2,1)S(1)}, u32[]{:S(2)}, u32[]{:S(2)}) collective-permute-start(bf16[4,128,384]{2,1,0:T(8,128)(2,1)S(1)} %pad_maximum_fusion.3.refs_4_), channel_id=1, source_target_pairs={{0,1},{1,0},{2,3},{3,2},{4,5},{5,4},{6,7},{7,6},{8,9},{9,8},{10,11... | collective-permute-start | bytes 1179656 | tf_op jit(solution)/shard_map/ppermute | solution.py:542
  111.9 72.2 %collective-permute-start.2 = (bf16[512,1024]{1,0:T(8,128)(2,1)}, bf16[512,1024]{1,0:T(8,128)(2,1)}, u32[]{:S(2)}, u32[]{:S(2)}) collective-permute-start(bf16[512,1024]{1,0:T(8,128)(2,1)} %collective-permute-done.1.refs_2_), channel_id=1, source_target_pairs={{0,8},{8,0},{16,24},{24,16},{1,9},{9,1},{17,25},{25,17},{2,10},{10... | collective-permute-start | bytes 3145736 | tf_op jit(solution)/shard_map/ppermute | solution.py:542
  175.8 31.8 %collective-permute-start.23 = (bf16[4,128,1280]{2,1,0:T(8,128)(2,1)S(1)}, bf16[4,128,1280]{2,1,0:T(8,128)(2,1)}, u32[]{:S(2)}, u32[]{:S(2)}) collective-permute-start(bf16[4,128,1280]{2,1,0:T(8,128)(2,1)S(1)} %pad_maximum_fusion.1.refs_10_), channel_id=1, source_target_pairs={{0,16},{8,24},{16,0},{24,8},{1,17},{9,25},{17,1},{25,9},{2,18},{10... | collective-permute-start | bytes 3932168 | tf_op jit(solution)/shard_map/ppermute | solution.py:542
  177.3 30.3 %collective-permute-start.21 = (bf16[4,128,1280]{2,1,0:T(8,128)(2,1)S(1)}, bf16[4,128,1280]{2,1,0:T(8,128)(2,1)}, u32[]{:S(2)}, u32[]{:S(2)}) collective-permute-start(bf16[4,128,1280]{2,1,0:T(8,128)(2,1)S(1)} %pad_maximum_fusion.1.refs_10_), channel_id=1, source_target_pairs={{0,8},{8,0},{16,24},{24,16},{1,9},{9,1},{17,25},{25,17},{2,10},{10... | collective-permute-start | bytes 3932168 | tf_op jit(solution)/shard_map/ppermute | solution.py:542
  182.6 16.4 %collective-permute-start.6 = (bf16[4,128,384]{2,1,0:T(8,128)(2,1)S(1)}, bf16[4,128,384]{2,1,0:T(8,128)(2,1)S(1)}, u32[]{:S(2)}, u32[]{:S(2)}) collective-permute-start(bf16[4,128,384]{2,1,0:T(8,128)(2,1)S(1)} %pad_maximum_fusion.2.refs_4_), channel_id=1, source_target_pairs={{0,1},{1,0},{2,3},{3,2},{4,5},{5,4},{6,7},{7,6},{8,9},{9,8},{10,11... | collective-permute-start | bytes 1179656 | tf_op jit(solution)/shard_map/ppermute | solution.py:542
  184.2 62.5 %collective-permute-start.24 = (bf16[4,128,1280]{2,1,0:T(8,128)(2,1)}, bf16[4,128,1280]{2,1,0:T(8,128)(2,1)}, u32[]{:S(2)}, u32[]{:S(2)}) collective-permute-start(bf16[4,128,1280]{2,1,0:T(8,128)(2,1)} %collective-permute-done.20.refs_11_), channel_id=1, source_target_pairs={{0,16},{8,24},{16,0},{24,8},{1,17},{9,25},{17,1},{25,9},{2,18},{10... | collective-permute-start | bytes 3932168 | tf_op jit(solution)/shard_map/ppermute | solution.py:542
  198.9 48.1 %collective-permute-start.31 = (bf16[4,256,1024]{2,1,0:T(8,128)(2,1)}, bf16[4,256,1024]{2,1,0:T(8,128)(2,1)S(1)}, u32[]{:S(2)}, u32[]{:S(2)}) collective-permute-start(bf16[4,256,1024]{2,1,0:T(8,128)(2,1)} %pad_maximum_fusion.refs_18_), channel_id=1, source_target_pairs={{0,8},{8,0},{16,24},{24,16},{1,9},{9,1},{17,25},{25,17},{2,10},{10... | collective-permute-start | bytes 6291464 | tf_op jit(solution)/shard_map/ppermute | solution.py:542
  207.6 16.0 %collective-permute-start.14 = (bf16[512,128]{1,0:T(8,128)(2,1)}, bf16[512,128]{1,0:T(8,128)(2,1)S(1)}, u32[]{:S(2)}, u32[]{:S(2)}) collective-permute-start(bf16[512,128]{1,0:T(8,128)(2,1)} %get-tuple-element.53.refs_7_), channel_id=1, source_target_pairs={{0,8},{8,0},{16,24},{24,16},{1,9},{9,1},{17,25},{25,17},{2,10},{10... | collective-permute-start | bytes 393224 | tf_op jit(solution)/shard_map/ppermute | solution.py:542
  207.6 29.4 %collective-permute-start.15 = (bf16[512,128]{1,0:T(8,128)(2,1)}, bf16[512,128]{1,0:T(8,128)(2,1)S(1)}, u32[]{:S(2)}, u32[]{:S(2)}) collective-permute-start(bf16[512,128]{1,0:T(8,128)(2,1)} %get-tuple-element.54.refs_8_), channel_id=1, source_target_pairs={{0,16},{8,24},{16,0},{24,8},{1,17},{9,25},{17,1},{25,9},{2,18},{10... | collective-permute-start | bytes 393224 | tf_op jit(solution)/shard_map/ppermute | solution.py:542
  209.1 42.6 %collective-permute-start.32 = (bf16[4,256,1024]{2,1,0:T(8,128)(2,1)}, bf16[4,256,1024]{2,1,0:T(8,128)(2,1)S(1)}, u32[]{:S(2)}, u32[]{:S(2)}) collective-permute-start(bf16[4,256,1024]{2,1,0:T(8,128)(2,1)} %collective-permute-done.30.refs_19_), channel_id=1, source_target_pairs={{0,8},{8,0},{16,24},{24,16},{1,9},{9,1},{17,25},{25,17},{2,10},{10... | collective-permute-start | bytes 6291464 | tf_op jit(solution)/shard_map/ppermute | solution.py:542
  223.7 13.8 %collective-permute-start.16 = (bf16[512,128]{1,0:T(8,128)(2,1)S(1)}, bf16[512,128]{1,0:T(8,128)(2,1)S(1)}, u32[]{:S(2)}, u32[]{:S(2)}) collective-permute-start(bf16[512,128]{1,0:T(8,128)(2,1)S(1)} %copy-done.51), channel_id=1, source_target_pairs={{0,24},{8,16},{16,8},{24,0},{1,25},{9,17},{17,9},{25,1},{2,26},{10... | collective-permute-start | bytes 393224 | tf_op jit(solution)/shard_map/ppermute | solution.py:542
  237.1 1.6 collective-permute-start.7
  237.5 6.6 %collective-permute-start.8 = (bf16[512,128]{1,0:T(8,128)(2,1)}, bf16[512,128]{1,0:T(8,128)(2,1)S(1)}, u32[]{:S(2)}, u32[]{:S(2)}) collective-permute-start(bf16[512,128]{1,0:T(8,128)(2,1)} %get-tuple-element.49.refs_8_), channel_id=1, source_target_pairs={{0,16},{8,24},{16,0},{24,8},{1,17},{9,25},{17,1},{25,9},{2,18},{10... | collective-permute-start | bytes 393224 | tf_op jit(solution)/shard_map/ppermute | solution.py:542
  238.7 7.9 %collective-permute-start.9 = (bf16[512,128]{1,0:T(8,128)(2,1)}, bf16[512,128]{1,0:T(8,128)(2,1)S(1)}, u32[]{:S(2)}, u32[]{:S(2)}) collective-permute-start(bf16[512,128]{1,0:T(8,128)(2,1)} %get-tuple-element.50.refs_9_), channel_id=1, source_target_pairs={{0,24},{8,16},{16,8},{24,0},{1,25},{9,17},{17,9},{25,1},{2,26},{10... | collective-permute-start | bytes 393224 | tf_op jit(solution)/shard_map/ppermute | solution.py:542
  244.1 3.2 collective-permute-start.22
  246.6 3.2 collective-permute-start.25
  246.7 5.0 %collective-permute-start.26 = (bf16[4,128,1280]{2,1,0:T(8,128)(2,1)}, bf16[4,128,1280]{2,1,0:T(8,128)(2,1)S(1)}, u32[]{:S(2)}, u32[]{:S(2)}) collective-permute-start(bf16[4,128,1280]{2,1,0:T(8,128)(2,1)} %collective-permute-done.24.refs_15_), channel_id=1, source_target_pairs={{0,8},{8,0},{16,24},{24,16},{1,9},{9,1},{17,25},{25,17},{2,10},{10... | collective-permute-start | bytes 3932168 | tf_op jit(solution)/shard_map/ppermute | solution.py:542
  287.3 3.8 collective-permute-start.33
  287.5 6.5 %collective-permute-start.34 = (bf16[512,128]{1,0:T(8,128)(2,1)}, bf16[512,128]{1,0:T(8,128)(2,1)S(1)}, u32[]{:S(2)}, u32[]{:S(2)}) collective-permute-start(bf16[512,128]{1,0:T(8,128)(2,1)} %get-tuple-element.64), channel_id=1, source_target_pairs={{0,16},{8,24},{16,0},{24,8},{1,17},{9,25},{17,1},{25,9},{2,18},{10... | collective-permute-start | bytes 393224 | tf_op jit(solution)/shard_map/ppermute | solution.py:542
  289.0 7.0 %collective-permute-start.35 = (bf16[512,128]{1,0:T(8,128)(2,1)}, bf16[512,128]{1,0:T(8,128)(2,1)S(1)}, u32[]{:S(2)}, u32[]{:S(2)}) collective-permute-start(bf16[512,128]{1,0:T(8,128)(2,1)} %get-tuple-element.65), channel_id=1, source_target_pairs={{0,24},{8,16},{16,8},{24,0},{1,25},{9,17},{17,9},{25,1},{2,26},{10... | collective-permute-start | bytes 393224 | tf_op jit(solution)/shard_map/ppermute | solution.py:542
  289.2 25.5 %collective-permute-start.36 = (bf16[512,128]{1,0:T(8,128)(2,1)}, bf16[512,128]{1,0:T(8,128)(2,1)S(1)}, u32[]{:S(2)}, u32[]{:S(2)}) collective-permute-start(bf16[512,128]{1,0:T(8,128)(2,1)} %get-tuple-element.71), channel_id=1, source_target_pairs={{0,8},{8,0},{16,24},{24,16},{1,9},{9,1},{17,25},{25,17},{2,10},{10... | collective-permute-start | bytes 393224 | tf_op jit(solution)/shard_map/ppermute | solution.py:542
  289.7 25.0 %collective-permute-start.37 = (bf16[512,128]{1,0:T(8,128)(2,1)}, bf16[512,128]{1,0:T(8,128)(2,1)S(1)}, u32[]{:S(2)}, u32[]{:S(2)}) collective-permute-start(bf16[512,128]{1,0:T(8,128)(2,1)} %get-tuple-element.72), channel_id=1, source_target_pairs={{0,16},{8,24},{16,0},{24,8},{1,17},{9,25},{17,1},{25,9},{2,18},{10... | collective-permute-start | bytes 393224 | tf_op jit(solution)/shard_map/ppermute | solution.py:542
  291.2 23.6 %collective-permute-start.38 = (bf16[512,128]{1,0:T(8,128)(2,1)}, bf16[512,128]{1,0:T(8,128)(2,1)S(1)}, u32[]{:S(2)}, u32[]{:S(2)}) collective-permute-start(bf16[512,128]{1,0:T(8,128)(2,1)} %get-tuple-element.73), channel_id=1, source_target_pairs={{0,24},{8,16},{16,8},{24,0},{1,25},{9,17},{17,9},{25,1},{2,26},{10... | collective-permute-start | bytes 393224 | tf_op jit(solution)/shard_map/ppermute | solution.py:542
  315.4 24.6 %copy-start.3 = (bf16[1024,384]{1,0:T(8,128)(2,1)S(1)}, bf16[1024,384]{1,0:T(8,128)(2,1)}, u32[]{:S(2)}) copy-start(bf16[1024,384]{1,0:T(8,128)(2,1)} %get-tuple-element.75) | copy-start | bytes 2359300
  334.4 16.7 %collective-permute-start.42 = (f32[2,16,2,128]{3,1,0,2:T(8,128)S(1)}, f32[2,16,2,128]{3,1,0,2:T(8,128)S(1)}, u32[]{:S(2)}, u32[]{:S(2)}) collective-permute-start(f32[2,16,2,128]{3,1,0,2:T(8,128)S(1)} %pad_maximum_fusion.4), channel_id=1, source_target_pairs={{0,4},{1,5},{2,6},{3,7},{4,0},{5,1},{6,2},{7,3},{8,12},{9,13},{10,... | collective-permute-start | bytes 98312 | tf_op jit(solution)/shard_map/ppermute | solution.py:542
  346.1 31.1 %collective-permute-start.40 = (bf16[512,1024]{1,0:T(8,128)(2,1)}, bf16[512,1024]{1,0:T(8,128)(2,1)}, u32[]{:S(2)}, u32[]{:S(2)}) collective-permute-start(bf16[512,1024]{1,0:T(8,128)(2,1)} %add_convert_fusion.1), channel_id=1, source_target_pairs={{0,8},{8,0},{16,24},{24,16},{1,9},{9,1},{17,25},{25,17},{2,10},{10... | collective-permute-start | bytes 3145736 | tf_op jit(solution)/shard_map/ppermute | solution.py:542
  351.1 10.2 %collective-permute-start.43 = (f32[2,16,2,128]{3,1,0,2:T(8,128)S(1)}, f32[2,16,2,128]{3,1,0,2:T(8,128)S(1)}, u32[]{:S(2)}, u32[]{:S(2)}) collective-permute-start(f32[2,16,2,128]{3,1,0,2:T(8,128)S(1)} %fusion.10), channel_id=1, source_target_pairs={{0,2},{1,3},{2,0},{3,1},{4,6},{5,7},{6,4},{7,5},{8,10},{9,11},{10,... | collective-permute-start | bytes 98312 | tf_op jit(solution)/shard_map/ppermute | solution.py:542
  361.2 4.0 collective-permute-start.44
  364.9 30.9 %collective-permute-start.39 = (bf16[512,1024]{1,0:T(8,128)(2,1)}, bf16[512,1024]{1,0:T(8,128)(2,1)S(1)}, u32[]{:S(2)}, u32[]{:S(2)}) collective-permute-start(bf16[512,1024]{1,0:T(8,128)(2,1)} %add_convert_fusion.2), channel_id=1, source_target_pairs={{0,8},{8,0},{16,24},{24,16},{1,9},{9,1},{17,25},{25,17},{2,10},{10... | collective-permute-start | bytes 3145736 | tf_op jit(solution)/shard_map/ppermute | solution.py:542
  365.2 2.4 collective-permute-start.45
  365.5 3.9 collective-permute-start.46
  369.4 1.2 collective-permute-start.47
  380.1 25.5 %collective-permute-start.41 = (bf16[512,1024]{1,0:T(8,128)(2,1)}, bf16[512,1024]{1,0:T(8,128)(2,1)}, u32[]{:S(2)}, u32[]{:S(2)}) collective-permute-start(bf16[512,1024]{1,0:T(8,128)(2,1)} %add_convert_fusion), channel_id=1, source_target_pairs={{0,16},{8,24},{16,0},{24,8},{1,17},{9,25},{17,1},{25,9},{2,18},{10... | collective-permute-start | bytes 3145736 | tf_op jit(solution)/shard_map/ppermute | solution.py:542
  (48 other events, 358.7 us)
